TPU v7x, 256 devices: a whole 4x4x8 slice. The times are simulated.
256 devices in a mesh: grp: 8 (over y, x_hi), shard: 32 (over z, x_lo, core).
Axes of the slice: x: 4 (x_hi: 2, x_lo: 2; x = x_hi * 2 + x_lo), y: 4, z: 8, core: 2. Of those that a mesh axis runs over, the one named last changes fastest.
Arguments:
- src: float32 [4096, 1024], P(('grp', 'shard')), may hold values from -64 to 64
- inv_src: float32 [4096], P(('grp', 'shard')), may hold values from 5 to 250
- tgt: float32 [32768, 1024], P(('shard', 'grp')), may hold values from -64 to 64
- inv_tgt: float32 [32768], P(('shard', 'grp')), may hold values from 5 to 250
Outputs:
- margin: float32 [4096, 32768], P('grp', 'shard')
All inputs are finite; a program needn't handle non-finite values.
Results may differ from a plain program's by a relative error of at most 0.00013.
Values sent between devices are 32-bit elements; how exact they have to be, the bound alone decides.
No kernel may reach another device: no remote copies, remote signals or barrier semaphores. Data moves between devices by JAX's collectives and lax.ppermute only.
A program may use at most 64 MiB of HBM per device.

v0:
```python
import functools
import math

import jax
import jax.numpy as jnp
from jax import lax
from jax.experimental import pallas as pl
from jax.experimental.pallas import tpu as pltpu
from jax.sharding import Mesh
from jax.sharding import PartitionSpec as P


FINE = ("y", "xh", "z", "xl", "c")
SRC = ("y", "xh", "z", "xl", "c")
TGT = ("z", "xl", "c", "y", "xh")
LANES = 128
NT = (((1,), (1,)), ((), ()))


CUT = 48
REST = LANES - CUT


def shifted(value, axis, by):
    n = lax.axis_size(axis)
    return lax.ppermute(value, axis, [(i, (i + by) % n) for i in range(n)])


def whole():
    return pl.BlockSpec(memory_space=pltpu.VMEM)


def first_kernel(src_ref, inv_ref, tgt_ref, tinv_ref, own_ref, q_ref, p_ref, rows, lane, tlane, sems):
    pairs = (
        (tgt_ref.at[CUT:], q_ref.at[:REST]),
        (tgt_ref.at[:CUT], p_ref),
        (src_ref, rows),
        (inv_ref, lane),
        (tinv_ref, tlane),
    )
    copies = [pltpu.make_async_copy(a, b, sems.at[k]) for k, (a, b) in enumerate(pairs)]
    for copy in copies:
        copy.start()
    q_ref[REST:, :] = jnp.zeros((8, 1024), jnp.float32)
    for copy in copies[2:]:
        copy.wait()
    for k in range(8):
        for r in range(2):
            at = r * 64 + k * 8
            own_ref[at : at + 8, :] = rows[r * 8 : r * 8 + 8, k * LANES : (k + 1) * LANES]
    same = lax.broadcasted_iota(jnp.int32, (16, 16), 0) == lax.broadcasted_iota(
        jnp.int32, (16, 16), 1
    )
    wide = jnp.where(same, jnp.broadcast_to(lane[...], (16, 16)), 0.0)
    own_ref[128:144, :] = jnp.broadcast_to(jnp.sum(wide, axis=1, keepdims=True), (16, LANES))
    q_ref[REST : REST + 1, :LANES] = tlane[...]
    for copy in copies[:2]:
        copy.wait()


def first_blocks(src, inv_src, tgt, inv_tgt):
    return pl.pallas_call(
        first_kernel,
        out_shape=(
            jax.ShapeDtypeStruct((144, LANES), jnp.float32),
            jax.ShapeDtypeStruct((REST + 8, 1024), jnp.float32),
            jax.ShapeDtypeStruct((CUT, 1024), jnp.float32),
        ),
        in_specs=[pl.BlockSpec(memory_space=pl.ANY)] * 4,
        out_specs=(whole(),) * 3,
        scratch_shapes=[
            pltpu.VMEM((16, 1024), jnp.float32),
            pltpu.VMEM((1, 16), jnp.float32),
            pltpu.VMEM((1, LANES), jnp.float32),
            pltpu.SemaphoreType.DMA((5,)),
        ],
        compiler_params=pltpu.CompilerParams(vmem_limit_bytes=60 << 20),
        cost_estimate=pl.CostEstimate(flops=1 << 16, bytes_accessed=1 << 20, transcendentals=0),
    )(src, inv_src[None, :], tgt, inv_tgt[None, :])


def rows_kernel(*refs):
    *groups, hi_ref, lo_ref, inv_ref = refs
    z, xl, c = lax.axis_index("z"), lax.axis_index("xl"), lax.axis_index("c")
    for (zs, dc), ref in zip(ROW_GROUPS, groups):
        at = 0
        for dz in zs:
            for dx in (0, 1):
                block = ref[at]
                at += 1
                place = lax.rem(z + dz + 8, 8) * 64 + (xl ^ dx) * 32 + (c ^ dc) * 16
                place = pl.multiple_of(place, 16)
                tiles = block[:128].reshape(2, 8, 8, LANES)
                square = jnp.sum(tiles * tiles, axis=1)
                total = jnp.sum(square, axis=-1, keepdims=True)
                scale = jnp.broadcast_to(lax.rsqrt(total + 1e-06), square.shape)
                for k in range(8):
                    unit = (tiles[:, k] * scale).reshape(16, LANES)
                    hi = unit.astype(jnp.bfloat16)
                    lo = (unit - hi.astype(jnp.float32)).astype(jnp.bfloat16)
                    hi_ref[pl.ds(place, 16), k * LANES : (k + 1) * LANES] = hi
                    lo_ref[pl.ds(place, 16), k * LANES : (k + 1) * LANES] = lo
                inv_ref[pl.ds(place, 16), :] = block[128:]


ROW_GROUPS = tuple((zs, dc) for dc in (0, 1) for zs in ((0, -2, 2, 4), (-1, -3, 1, 3)))


def rows_ready(groups):
    return pl.pallas_call(
        rows_kernel,
        out_shape=(
            jax.ShapeDtypeStruct((512, 1024), jnp.bfloat16),
            jax.ShapeDtypeStruct((512, 1024), jnp.bfloat16),
            jax.ShapeDtypeStruct((512, LANES), jnp.float32),
        ),
        in_specs=[whole()] * len(groups),
        out_specs=(whole(),) * 3,
        compiler_params=pltpu.CompilerParams(vmem_limit_bytes=16 << 20),
        cost_estimate=pl.CostEstimate(flops=8 << 20, bytes_accessed=5 << 20, transcendentals=0),
    )(*groups)


def to_lanes(column):
    same = lax.broadcasted_iota(jnp.int32, (LANES, LANES), 0) == lax.broadcasted_iota(
        jnp.int32, (LANES, LANES), 1
    )
    wide = jnp.broadcast_to(column, (512, LANES)).reshape(4, LANES, LANES)
    return jnp.sum(jnp.where(same[None], wide, 0.0), axis=1)


def from_lanes(lines):
    same = lax.broadcasted_iota(jnp.int32, (LANES, LANES), 0) == lax.broadcasted_iota(
        jnp.int32, (LANES, LANES), 1
    )
    wide = jnp.broadcast_to(lines[:, None, :], (4, LANES, LANES))
    return jnp.sum(jnp.where(same[None], wide, 0.0), axis=2).reshape(512, 1)


LAYOUTS = (((LANES,),) * 4, ((CUT, REST),) * 4)


def tile_kernel(side, *refs):
    n = sum(len(parts) for parts in LAYOUTS[side])
    pieces, refs = refs[:n], refs[n:]
    hi_ref, lo_ref, inv_ref, *refs = refs
    y = lax.axis_index("y")
    if side == 1:
        before_ref, before_sims, *refs = refs
        tails, refs = refs[:4], refs[4:]
        sims_ref, row_ref, col_ref, tinv_ref, bhi, blo = refs
        for dy, tail in zip((0, -1, 1, 2), tails):
            spot = lax.rem(y + dy + 4, 4)
            tinv_ref[pl.ds(spot, 1), :] = tail[1:2, :]
            tinv_ref[pl.ds(spot + 4, 1), :] = tail[0:1, :]
    else:
        sims_ref, row_ref, bhi, blo = refs
    k = 0
    for dy, parts in zip((0, -1, 1, 2), LAYOUTS[side]):
        spot = lax.rem(y + dy + 4, 4)
        at = 0
        for rows in parts:
            value = pieces[k][:rows, :]
            k += 1
            total = jnp.sum(value * value, axis=1, keepdims=True)
            unit = value * lax.rsqrt(total + 1e-06)
            hi = unit.astype(jnp.bfloat16)
            place = pl.ds(pl.multiple_of(spot * LANES + at, 8), rows)
            bhi[place, :] = hi
            blo[place, :] = (unit - hi.astype(jnp.float32)).astype(jnp.bfloat16)
            at += rows
    dot = functools.partial(lax.dot_general, preferred_element_type=jnp.float32)
    sims = dot(hi_ref[...], bhi[...], NT)
    sims += dot(hi_ref[...], blo[...], NT)
    sims += dot(lo_ref[...], bhi[...], NT)
    sims_ref[...] = sims
    inv = inv_ref[:, :1]
    logits = sims * inv
    top = jnp.max(logits, axis=1, keepdims=True)
    total = jnp.sum(jnp.exp(logits - top), axis=1, keepdims=True)
    lines_top, lines_total = to_lanes(top), to_lanes(total)
    if side == 1:
        other_top, other_total = before_ref[0:4, :], before_ref[4:8, :]
        best = jnp.maximum(lines_top, other_top)
        lines_total = lines_total * jnp.exp(lines_top - best) + other_total * jnp.exp(other_top - best)
        lines_top = best
    row_ref[0:4, :] = lines_top
    row_ref[4:8, :] = lines_total
    if side == 1:
        for j in range(8):
            k = (j % 4) * LANES
            part = before_sims[:, k : k + LANES] if j < 4 else sims[:, k : k + LANES]
            logits = part * tinv_ref[j : j + 1, :]
            top = jnp.max(logits, axis=0, keepdims=True)
            col_ref[j : j + 1, :] = top
            col_ref[8 + j : 9 + j, :] = jnp.sum(jnp.exp(logits - top), axis=0, keepdims=True)


def tile(side, pieces, *operands):
    operands = (*pieces, *operands)
    shapes = [
        jax.ShapeDtypeStruct((512, 512), jnp.float32),
        jax.ShapeDtypeStruct((8, LANES), jnp.float32),
    ]
    if side == 1:
        shapes += [
            jax.ShapeDtypeStruct((16, LANES), jnp.float32),
            jax.ShapeDtypeStruct((8, LANES), jnp.float32),
        ]
    return pl.pallas_call(
        functools.partial(tile_kernel, side),
        out_shape=shapes,
        in_specs=[whole()] * len(operands),
        out_specs=[whole()] * len(shapes),
        scratch_shapes=[pltpu.VMEM((512, 1024), jnp.bfloat16)] * 2,
        compiler_params=pltpu.CompilerParams(vmem_limit_bytes=24 << 20),
        cost_estimate=pl.CostEstimate(
            flops=3 << 29, bytes_accessed=6 << 20, transcendentals=1 << 19
        ),
    )(*operands)


def final_kernel(same_ref, other_ref, inv_ref, tinv_ref, row_ref, col_ref, out_ref):
    xh = lax.axis_index("xh")
    row = from_lanes(row_ref[0:4, :] + jnp.log(row_ref[4:8, :])) - math.log(32768)
    inv = inv_ref[:, :1]
    col = col_ref[0:8, :] + jnp.log(col_ref[8:16, :]) - math.log(4096)
    for side, sims_ref in enumerate((same_ref, other_ref)):
        for j in range(4):
            place = pl.multiple_of((2 * j + (xh ^ side)) * LANES, LANES)
            right = col[4 * side + j : 4 * side + j + 1, :]
            top = jnp.maximum(row, right)
            gap = jnp.minimum(row, right) - top
            both = top + jnp.log(1.0 + jnp.exp(gap)) - math.log(2.0)
            scale = 0.5 * (inv + tinv_ref[4 * side + j : 4 * side + j + 1, :])
            sims = sims_ref[:, j * LANES : (j + 1) * LANES]
            out_ref[:, pl.ds(place, LANES)] = sims * scale - both


def final(*operands):
    return pl.pallas_call(
        final_kernel,
        out_shape=jax.ShapeDtypeStruct((512, 1024), jnp.float32),
        in_specs=[whole()] * 6,
        out_specs=whole(),
        compiler_params=pltpu.CompilerParams(vmem_limit_bytes=24 << 20),
    )(*operands)


def joined(values):
    half = values[0].shape[0] // 2
    best = functools.reduce(jnp.maximum, [v[:half] for v in values])
    total = sum(v[half:] * jnp.exp(v[:half] - best) for v in values)
    return jnp.concatenate([best, total])


def gathered_rows(own):
    pair = jnp.stack([own, shifted(own, "xl", 1)])
    below = shifted(pair, "z", 2)
    above = shifted(pair, "z", -2)
    across = shifted(pair, "z", 4)
    down = shifted(jnp.concatenate([pair, below]), "z", 1)
    up = shifted(jnp.concatenate([pair, above]), "z", -1)
    near = jnp.concatenate([pair, below, above, across])
    rest = jnp.concatenate([down, up])
    return near, rest, shifted(near, "c", 1), shifted(rest, "c", 1)


def gathered_columns(tgt, inv_tgt, q, p):
    down = shifted(tgt, "y", 1)
    up = shifted(tgt, "y", -1)
    far = shifted(tgt, "y", 2)
    q = shifted(q, "xh", 1)
    q_own = shifted(p, "xh", 1)
    tail = [inv_tgt[None, :], jnp.zeros((6, LANES), jnp.float32)]
    tail = jnp.pad(jnp.concatenate(tail), ((0, 0), (0, 1024 - LANES)))
    q = jnp.concatenate([q[: REST + 1], tail])
    q_down = shifted(q, "y", 1)
    q_up = shifted(q, "y", -1)
    q_far = shifted(q, "y", 2)
    both = jnp.concatenate([down[:CUT], up[:CUT]])
    q_both = shifted(both, "xh", 1)
    q_f = shifted(far[:CUT], "xh", 1)
    same = (tgt, down, up, far)
    other = (q_own, q, q_both[:CUT], q_down, q_both[CUT:], q_up, q_f, q_far)
    return same, other, tuple(v[REST : REST + 2, :LANES] for v in (q, q_down, q_up, q_far))


def all_rows(row):
    row = joined([row, shifted(row, "c", 1)])
    row = joined([row] + [shifted(row, "z", k) for k in (2, -2, 4)])
    flip = [(i, i ^ 1) for i in range(8)]
    beside = lax.ppermute(row, "z", flip)
    crossed = lax.ppermute(
        row, ("z", "xl"), [(2 * i + k, 2 * (i ^ 1) + (k ^ 1)) for i in range(8) for k in range(2)]
    )
    return joined([row, beside, shifted(row, "xl", 1), crossed])


def all_columns(col):
    col = joined([col] + [shifted(col, "y", k) for k in (1, -1, 2)])
    over = shifted(col, "xh", 1)
    return joined([col, jnp.concatenate([over[4:8], over[0:4], over[12:16], over[8:12]])])


def body(src, inv_src, tgt, inv_tgt):
    own, q, p = first_blocks(src, inv_src, tgt, inv_tgt)
    same, other, tails = gathered_columns(tgt, inv_tgt, q, p)
    blocks = gathered_rows(own)
    hi, lo, inv = rows_ready(blocks)
    sims_same, row = tile(0, same, hi, lo, inv)
    sims_other, row, col, tinv = tile(1, other, hi, lo, inv, row, sims_same, *tails)
    col = all_columns(col)
    row = all_rows(row)
    return final(sims_same, sims_other, inv, tinv, row, col)


def solution(mesh):
    finer = Mesh(mesh.devices.reshape(4, 2, 8, 2, 2), FINE)
    placed = (P(SRC, None), P(SRC), P(TGT, None), P(TGT))
    return jax.shard_map(
        body,
        mesh=finer,
        in_specs=placed,
        out_specs=P(("y", "xh"), ("z", "xl", "c")),
        check_vma=False,
    )
```

profile of v0, /device:TPU:2, one launch (start us, length us, event | category | flops | bytes accessed | tf_op | source)
XLA Modules:
  0.0 103.5 jit_solution(10892379710040099368)
XLA Ops:
  1.6 1.7 %collective-permute-start.1 = (f32[128,1024]{1,0:T(8,128)}, f32[128,1024]{1,0:T(8,128)S(1)}, u32[]{:S(2)}, u32[]{:S(2)}) collective-permute-start(f32[128,1024]{1,0:T(8,128)} %refs_0_.1), channel_id=1, source_target_pairs={{0,192},{64,0},{128,64},{192,128},{1,193},{65,1},{129,65},{193,129... | collective-permute-start | bytes 1572872 | tf_op jit(solution)/shard_map/ppermute | solution.py:26
  3.2 2.0 %shard_map.46 = (f32[144,128]{1,0:T(8,128)}, f32[88,1024]{1,0:T(8,128)}, f32[48,1024]{1,0:T(8,128)}) custom-call(f32[16,1024]{1,0:T(8,128)} %src_ref.1, f32[1,16]{1,0:T(1,128)} %bitcast.14, f32[128,1024]{1,0:T(8,128)} %refs_0_.1, f32[1,128]{1,0:T(1,128)} %bitcast.12), custom_call_target="tpu_custom_call" | custom-call | flops 65536 | bytes 1048576 | tf_op jit(solution)/shard_map/pallas_call | solution.py:62
  5.2 2.3 %collective-permute-start.3 = (f32[144,128]{1,0:T(8,128)}, f32[144,128]{1,0:T(8,128)S(1)}, u32[]{:S(2)}, u32[]{:S(2)}) collective-permute-start(f32[144,128]{1,0:T(8,128)} %get-tuple-element.17), channel_id=1, source_target_pairs={{0,2},{2,0},{1,3},{3,1},{4,6},{6,4},{5,7},{7,5},{8,10},{10,8},{9,1... | collective-permute-start | bytes 221192 | tf_op jit(solution)/shard_map/ppermute | solution.py:26
  11.4 2.7 %collective-permute-start.4 = (f32[2,144,128]{2,1,0:T(8,128)S(1)}, f32[2,144,128]{2,1,0:T(8,128)S(1)}, u32[]{:S(2)}, u32[]{:S(2)}) collective-permute-start(f32[2,144,128]{2,1,0:T(8,128)S(1)} %pad_maximum_fusion.3), channel_id=1, source_target_pairs={{0,8},{4,12},{8,16},{12,20},{16,24},{20,28},{24,0},{28,4},{1,9},{5... | collective-permute-start | bytes 442376 | tf_op jit(solution)/shard_map/ppermute | solution.py:26
  14.1 3.1 %collective-permute-start.5 = (f32[2,144,128]{2,1,0:T(8,128)S(1)}, f32[2,144,128]{2,1,0:T(8,128)S(1)}, u32[]{:S(2)}, u32[]{:S(2)}) collective-permute-start(f32[2,144,128]{2,1,0:T(8,128)S(1)} %pad_maximum_fusion.3), channel_id=1, source_target_pairs={{0,24},{4,28},{8,0},{12,4},{16,8},{20,12},{24,16},{28,20},{1,25},{... | collective-permute-start | bytes 442376 | tf_op jit(solution)/shard_map/ppermute | solution.py:26
  17.3 3.1 %collective-permute-done.4 = f32[2,144,128]{2,1,0:T(8,128)S(1)} collective-permute-done((f32[2,144,128]{2,1,0:T(8,128)S(1)}, f32[2,144,128]{2,1,0:T(8,128)S(1)}, u32[]{:S(2)}, u32[]{:S(2)}) %collective-permute-start.4) | collective-permute-done | bytes 147488 | tf_op jit(solution)/shard_map/ppermute | solution.py:26
  20.4 6.8 %collective-permute-start.6 = (f32[2,144,128]{2,1,0:T(8,128)S(1)}, f32[2,144,128]{2,1,0:T(8,128)S(1)}, u32[]{:S(2)}, u32[]{:S(2)}) collective-permute-start(f32[2,144,128]{2,1,0:T(8,128)S(1)} %pad_maximum_fusion.3), channel_id=1, source_target_pairs={{0,16},{4,20},{8,24},{12,28},{16,0},{20,4},{24,8},{28,12},{1,17},{... | collective-permute-start | bytes 442376 | tf_op jit(solution)/shard_map/ppermute | solution.py:26
  28.3 4.3 %collective-permute-done.6 = f32[2,144,128]{2,1,0:T(8,128)S(1)} collective-permute-done((f32[2,144,128]{2,1,0:T(8,128)S(1)}, f32[2,144,128]{2,1,0:T(8,128)S(1)}, u32[]{:S(2)}, u32[]{:S(2)}) %collective-permute-start.6) | collective-permute-done | bytes 147488 | tf_op jit(solution)/shard_map/ppermute | solution.py:26
  32.6 1.6 %collective-permute-start.2 = (f32[128,1024]{1,0:T(8,128)S(1)}, f32[128,1024]{1,0:T(8,128)S(1)}, u32[]{:S(2)}, u32[]{:S(2)}) collective-permute-start(f32[128,1024]{1,0:T(8,128)S(1)} %copy-done), channel_id=1, source_target_pairs={{0,128},{64,192},{128,0},{192,64},{1,129},{65,193},{129,1},{193,65... | collective-permute-start | bytes 1572872 | tf_op jit(solution)/shard_map/ppermute | solution.py:26
  34.2 5.0 %collective-permute-start.8 = (f32[4,144,128]{2,1,0:T(8,128)S(1)}, f32[4,144,128]{2,1,0:T(8,128)S(1)}, u32[]{:S(2)}, u32[]{:S(2)}) collective-permute-start(f32[4,144,128]{2,1,0:T(8,128)S(1)} %get-tuple-element.39), channel_id=1, source_target_pairs={{0,28},{4,0},{8,4},{12,8},{16,12},{20,16},{24,20},{28,24},{1,29},{... | collective-permute-start | bytes 884744 | tf_op jit(solution)/shard_map/ppermute | solution.py:26
  40.4 2.2 %collective-permute-start.15 = (f32[88,1024]{1,0:T(8,128)S(1)}, f32[88,1024]{1,0:T(8,128)S(1)}, u32[]{:S(2)}, u32[]{:S(2)}) collective-permute-start(f32[88,1024]{1,0:T(8,128)S(1)} %select_maximum_fusion.refs_1_), channel_id=1, source_target_pairs={{0,192},{64,0},{128,64},{192,128},{1,193},{65,1},{129,65},{193,129... | collective-permute-start | bytes 1081352 | tf_op jit(solution)/shard_map/ppermute | solution.py:26
  43.4 2.4 %collective-permute-start.13 = (f32[96,1024]{1,0:T(8,128)S(1)}, f32[96,1024]{1,0:T(8,128)S(1)}, u32[]{:S(2)}, u32[]{:S(2)}) collective-permute-start(f32[96,1024]{1,0:T(8,128)S(1)} %pad_maximum_fusion), channel_id=1, source_target_pairs={{0,32},{32,0},{1,33},{33,1},{2,34},{34,2},{3,35},{35,3},{4,36},{36... | collective-permute-start | bytes 1179656 | tf_op jit(solution)/shard_map/ppermute | solution.py:26
  46.6 12.3 %collective-permute-done.14.refs_3_ = f32[88,1024]{1,0:T(8,128)S(1)} collective-permute-done((f32[88,1024]{1,0:T(8,128)S(1)}, f32[88,1024]{1,0:T(8,128)S(1)}, u32[]{:S(2)}, u32[]{:S(2)}) %collective-permute-start.14) | collective-permute-done | bytes 360480 | tf_op jit(solution)/shard_map/ppermute | solution.py:26
  59.0 2.7 %collective-permute-start.11 = (f32[48,1024]{1,0:T(8,128)S(1)}, f32[48,1024]{1,0:T(8,128)S(1)}, u32[]{:S(2)}, u32[]{:S(2)}) collective-permute-start(f32[48,1024]{1,0:T(8,128)S(1)} %copy-done.2), channel_id=1, source_target_pairs={{0,32},{32,0},{1,33},{33,1},{2,34},{34,2},{3,35},{35,3},{4,36},{36... | collective-permute-start | bytes 589832 | tf_op jit(solution)/shard_map/ppermute | solution.py:26
  63.5 2.6 %shard_map.48 = (f32[512,512]{1,0:T(8,128)S(1)}, f32[8,128]{1,0:T(8,128)S(1)}) custom-call(f32[128,1024]{1,0:T(8,128)S(1)} %copy-done, f32[128,1024]{1,0:T(8,128)S(1)} %collective-permute-done.refs_1_, f32[128,1024]{1,0:T(8,128)S(1)} %collective-permute-done.1.refs_2_, f32[128,1024]{1,0:T(8,128)S(1)} %collective-permute-done.2.refs_3_, ...), custom_call_target="tpu_custom_call" | custom-call | flops 1610612736 | bytes 6291456 | tf_op jit(solution)/shard_map/pallas_call | solution.py:210
  66.2 2.2 %collective-permute-done.11.refs_0_ = f32[48,1024]{1,0:T(8,128)S(1)} collective-permute-done((f32[48,1024]{1,0:T(8,128)S(1)}, f32[48,1024]{1,0:T(8,128)S(1)}, u32[]{:S(2)}, u32[]{:S(2)}) %collective-permute-start.11) | collective-permute-done | bytes 196640 | tf_op jit(solution)/shard_map/ppermute | solution.py:26
  68.3 3.8 %collective-permute-done.16.refs_6_ = f32[48,1024]{1,0:T(8,128)S(1)} collective-permute-done((f32[48,1024]{1,0:T(8,128)S(1)}, f32[48,1024]{1,0:T(8,128)S(1)}, u32[]{:S(2)}, u32[]{:S(2)}) %collective-permute-start.16) | collective-permute-done | bytes 196640 | tf_op jit(solution)/shard_map/ppermute | solution.py:26
  72.1 3.1 %shard_map.49 = (f32[512,512]{1,0:T(8,128)S(1)}, f32[8,128]{1,0:T(8,128)S(1)}, f32[16,128]{1,0:T(8,128)S(1)}, f32[8,128]{1,0:T(8,128)S(1)}) custom-call(f32[48,1024]{1,0:T(8,128)S(1)} %collective-permute-done.11.refs_0_, f32[88,1024]{1,0:T(8,128)S(1)} %select_maximum_fusion.refs_1_, f32[48,1024]{1,0:T(8,128)S(1)} %get-tuple-element.38.refs_2_, ...), custom_call_target="tpu_custom_call" | custom-call | flops 1610612736 | bytes 6291456 | tf_op jit(solution)/shard_map/pallas_call | solution.py:210
  76.6 4.1 %collective-permute-start.20 = (f32[8,128]{1,0:T(8,128)S(1)}, f32[8,128]{1,0:T(8,128)S(1)}, u32[]{:S(2)}, u32[]{:S(2)}) collective-permute-start(f32[8,128]{1,0:T(8,128)S(1)} %pad_maximum_fusion.6), channel_id=1, source_target_pairs={{0,24},{4,28},{8,0},{12,4},{16,8},{20,12},{24,16},{28,20},{1,25},{... | collective-permute-start | bytes 12296 | tf_op jit(solution)/shard_map/ppermute | solution.py:26
  80.7 6.4 %collective-permute-start.21 = (f32[8,128]{1,0:T(8,128)S(1)}, f32[8,128]{1,0:T(8,128)S(1)}, u32[]{:S(2)}, u32[]{:S(2)}) collective-permute-start(f32[8,128]{1,0:T(8,128)S(1)} %pad_maximum_fusion.6), channel_id=1, source_target_pairs={{0,16},{4,20},{8,24},{12,28},{16,0},{20,4},{24,8},{28,12},{1,17},{... | collective-permute-start | bytes 12296 | tf_op jit(solution)/shard_map/ppermute | solution.py:26
  87.2 3.2 %collective-permute-start.26 = (f32[16,128]{1,0:T(8,128)S(1)}, f32[16,128]{1,0:T(8,128)S(1)}, u32[]{:S(2)}, u32[]{:S(2)}) collective-permute-start(f32[16,128]{1,0:T(8,128)S(1)} %get-tuple-element.28), channel_id=1, source_target_pairs={{0,192},{64,0},{128,64},{192,128},{1,193},{65,1},{129,65},{193,129... | collective-permute-start | bytes 24584 | tf_op jit(solution)/shard_map/ppermute | solution.py:26
  92.2 1.9 %collective-permute-start.24 = (f32[8,128]{1,0:T(8,128)S(1)}, f32[8,128]{1,0:T(8,128)S(1)}, u32[]{:S(2)}, u32[]{:S(2)}) collective-permute-start(f32[8,128]{1,0:T(8,128)S(1)} %pad_maximum_fusion.7), channel_id=1, source_target_pairs={{0,6},{2,4},{4,2},{6,0},{8,14},{10,12},{12,10},{14,8},{16,22},{18,... | collective-permute-start | bytes 12296 | tf_op jit(solution)/shard_map/ppermute | solution.py:294
  96.7 4.1 %collective-permute-done.28 = f32[16,128]{1,0:T(8,128)S(1)} collective-permute-done((f32[16,128]{1,0:T(8,128)S(1)}, f32[16,128]{1,0:T(8,128)S(1)}, u32[]{:S(2)}, u32[]{:S(2)}) %collective-permute-start.28) | collective-permute-done | bytes 8224 | tf_op jit(solution)/shard_map/ppermute | solution.py:26
  100.8 2.7 %shard_map.50 = f32[512,1024]{1,0:T(8,128)} custom-call(f32[512,512]{1,0:T(8,128)S(1)} %get-tuple-element.21.refs_12_.same_ref, f32[512,512]{1,0:T(8,128)S(1)} %get-tuple-element.25.other_ref, f32[512,128]{1,0:T(8,128)S(1)} %get-tuple-element.20.refs_6_.refs_10_.inv_ref, f32[8,128]{1,0:T(8,128)S(1)} %get-tuple-element.26.tinv_ref, ...), custom_call_target="tpu_custom_call" | custom-call | tf_op jit(solution)/shard_map/pallas_call | solution.py:241
  (75 shorter events, 17.0 us)
Async XLA Ops:
  0.0 40.4 %collective-permute-start = (f32[128,1024]{1,0:T(8,128)}, f32[128,1024]{1,0:T(8,128)S(1)}, u32[]{:S(2)}, u32[]{:S(2)}) collective-permute-start(f32[128,1024]{1,0:T(8,128)} %refs_0_.1), channel_id=1, source_target_pairs={{0,64},{64,128},{128,192},{192,0},{1,65},{65,129},{129,193},{193,1... | collective-permute-start | bytes 1572872 | tf_op jit(solution)/shard_map/ppermute | solution.py:26
  1.6 41.1 %collective-permute-start.1 = (f32[128,1024]{1,0:T(8,128)}, f32[128,1024]{1,0:T(8,128)S(1)}, u32[]{:S(2)}, u32[]{:S(2)}) collective-permute-start(f32[128,1024]{1,0:T(8,128)} %refs_0_.1), channel_id=1, source_target_pairs={{0,192},{64,0},{128,64},{192,128},{1,193},{65,1},{129,65},{193,129... | collective-permute-start | bytes 1572872 | tf_op jit(solution)/shard_map/ppermute | solution.py:26
  5.2 5.3 %collective-permute-start.3 = (f32[144,128]{1,0:T(8,128)}, f32[144,128]{1,0:T(8,128)S(1)}, u32[]{:S(2)}, u32[]{:S(2)}) collective-permute-start(f32[144,128]{1,0:T(8,128)} %get-tuple-element.17), channel_id=1, source_target_pairs={{0,2},{2,0},{1,3},{3,1},{4,6},{6,4},{5,7},{7,5},{8,10},{10,8},{9,1... | collective-permute-start | bytes 221192 | tf_op jit(solution)/shard_map/ppermute | solution.py:26
  7.6 26.6 %collective-permute-start.12 = (f32[88,1024]{1,0:T(8,128)}, f32[88,1024]{1,0:T(8,128)S(1)}, u32[]{:S(2)}, u32[]{:S(2)}) collective-permute-start(f32[88,1024]{1,0:T(8,128)} %get-tuple-element.23), channel_id=1, source_target_pairs={{0,32},{32,0},{1,33},{33,1},{2,34},{34,2},{3,35},{35,3},{4,36},{36... | collective-permute-start | bytes 1081352 | tf_op jit(solution)/shard_map/ppermute | solution.py:26
  11.4 8.9 %collective-permute-start.4 = (f32[2,144,128]{2,1,0:T(8,128)S(1)}, f32[2,144,128]{2,1,0:T(8,128)S(1)}, u32[]{:S(2)}, u32[]{:S(2)}) collective-permute-start(f32[2,144,128]{2,1,0:T(8,128)S(1)} %pad_maximum_fusion.3), channel_id=1, source_target_pairs={{0,8},{4,12},{8,16},{12,20},{16,24},{20,28},{24,0},{28,4},{1,9},{5... | collective-permute-start | bytes 442376 | tf_op jit(solution)/shard_map/ppermute | solution.py:26
  14.1 13.1 %collective-permute-start.5 = (f32[2,144,128]{2,1,0:T(8,128)S(1)}, f32[2,144,128]{2,1,0:T(8,128)S(1)}, u32[]{:S(2)}, u32[]{:S(2)}) collective-permute-start(f32[2,144,128]{2,1,0:T(8,128)S(1)} %pad_maximum_fusion.3), channel_id=1, source_target_pairs={{0,24},{4,28},{8,0},{12,4},{16,8},{20,12},{24,16},{28,20},{1,25},{... | collective-permute-start | bytes 442376 | tf_op jit(solution)/shard_map/ppermute | solution.py:26
  20.4 12.2 %collective-permute-start.6 = (f32[2,144,128]{2,1,0:T(8,128)S(1)}, f32[2,144,128]{2,1,0:T(8,128)S(1)}, u32[]{:S(2)}, u32[]{:S(2)}) collective-permute-start(f32[2,144,128]{2,1,0:T(8,128)S(1)} %pad_maximum_fusion.3), channel_id=1, source_target_pairs={{0,16},{4,20},{8,24},{12,28},{16,0},{20,4},{24,8},{28,12},{1,17},{... | collective-permute-start | bytes 442376 | tf_op jit(solution)/shard_map/ppermute | solution.py:26
  28.1 11.1 %collective-permute-start.7 = (f32[4,144,128]{2,1,0:T(8,128)S(1)}, f32[4,144,128]{2,1,0:T(8,128)S(1)}, u32[]{:S(2)}, u32[]{:S(2)}) collective-permute-start(f32[4,144,128]{2,1,0:T(8,128)S(1)} %get-tuple-element.40), channel_id=1, source_target_pairs={{0,4},{4,8},{8,12},{12,16},{16,20},{20,24},{24,28},{28,0},{1,5},{5... | collective-permute-start | bytes 884744 | tf_op jit(solution)/shard_map/ppermute | solution.py:26
  32.6 14.1 %collective-permute-start.2 = (f32[128,1024]{1,0:T(8,128)S(1)}, f32[128,1024]{1,0:T(8,128)S(1)}, u32[]{:S(2)}, u32[]{:S(2)}) collective-permute-start(f32[128,1024]{1,0:T(8,128)S(1)} %copy-done), channel_id=1, source_target_pairs={{0,128},{64,192},{128,0},{192,64},{1,129},{65,193},{129,1},{193,65... | collective-permute-start | bytes 1572872 | tf_op jit(solution)/shard_map/ppermute | solution.py:26
  34.2 9.2 %collective-permute-start.8 = (f32[4,144,128]{2,1,0:T(8,128)S(1)}, f32[4,144,128]{2,1,0:T(8,128)S(1)}, u32[]{:S(2)}, u32[]{:S(2)}) collective-permute-start(f32[4,144,128]{2,1,0:T(8,128)S(1)} %get-tuple-element.39), channel_id=1, source_target_pairs={{0,28},{4,0},{8,4},{12,8},{16,12},{20,16},{24,20},{28,24},{1,29},{... | collective-permute-start | bytes 884744 | tf_op jit(solution)/shard_map/ppermute | solution.py:26
  39.2 19.7 %collective-permute-start.14 = (f32[88,1024]{1,0:T(8,128)S(1)}, f32[88,1024]{1,0:T(8,128)S(1)}, u32[]{:S(2)}, u32[]{:S(2)}) collective-permute-start(f32[88,1024]{1,0:T(8,128)S(1)} %select_maximum_fusion.refs_1_), channel_id=1, source_target_pairs={{0,64},{64,128},{128,192},{192,0},{1,65},{65,129},{129,193},{193,1... | collective-permute-start | bytes 1081352 | tf_op jit(solution)/shard_map/ppermute | solution.py:26
  40.4 18.5 %collective-permute-start.15 = (f32[88,1024]{1,0:T(8,128)S(1)}, f32[88,1024]{1,0:T(8,128)S(1)}, u32[]{:S(2)}, u32[]{:S(2)}) collective-permute-start(f32[88,1024]{1,0:T(8,128)S(1)} %select_maximum_fusion.refs_1_), channel_id=1, source_target_pairs={{0,192},{64,0},{128,64},{192,128},{1,193},{65,1},{129,65},{193,129... | collective-permute-start | bytes 1081352 | tf_op jit(solution)/shard_map/ppermute | solution.py:26
  42.6 19.0 %collective-permute-start.17 = (f32[88,1024]{1,0:T(8,128)S(1)}, f32[88,1024]{1,0:T(8,128)S(1)}, u32[]{:S(2)}, u32[]{:S(2)}) collective-permute-start(f32[88,1024]{1,0:T(8,128)S(1)} %select_maximum_fusion.refs_1_), channel_id=1, source_target_pairs={{0,128},{64,192},{128,0},{192,64},{1,129},{65,193},{129,1},{193,65... | collective-permute-start | bytes 1081352 | tf_op jit(solution)/shard_map/ppermute | solution.py:26
  43.4 19.5 %collective-permute-start.13 = (f32[96,1024]{1,0:T(8,128)S(1)}, f32[96,1024]{1,0:T(8,128)S(1)}, u32[]{:S(2)}, u32[]{:S(2)}) collective-permute-start(f32[96,1024]{1,0:T(8,128)S(1)} %pad_maximum_fusion), channel_id=1, source_target_pairs={{0,32},{32,0},{1,33},{33,1},{2,34},{34,2},{3,35},{35,3},{4,36},{36... | collective-permute-start | bytes 1179656 | tf_op jit(solution)/shard_map/ppermute | solution.py:26
  46.6 16.3 %collective-permute-start.9 = (f32[8,144,128]{2,1,0:T(8,128)S(1)}, f32[8,144,128]{2,1,0:T(8,128)S(1)}, u32[]{:S(2)}, u32[]{:S(2)}) collective-permute-start(f32[8,144,128]{2,1,0:T(8,128)S(1)} %constant_dynamic-update-slice_fusion.refs_0_), channel_id=1, source_target_pairs={{0,1},{1,0},{2,3},{3,2},{4,5},{5,4},{6,7},{7,6},{8,9},{9,8},{10,11... | collective-permute-start | bytes 1769480 | tf_op jit(solution)/shard_map/ppermute | solution.py:26
  59.0 9.4 %collective-permute-start.11 = (f32[48,1024]{1,0:T(8,128)S(1)}, f32[48,1024]{1,0:T(8,128)S(1)}, u32[]{:S(2)}, u32[]{:S(2)}) collective-permute-start(f32[48,1024]{1,0:T(8,128)S(1)} %copy-done.2), channel_id=1, source_target_pairs={{0,32},{32,0},{1,33},{33,1},{2,34},{34,2},{3,35},{35,3},{4,36},{36... | collective-permute-start | bytes 589832 | tf_op jit(solution)/shard_map/ppermute | solution.py:26
  61.7 10.4 %collective-permute-start.16 = (f32[48,1024]{1,0:T(8,128)S(1)}, f32[48,1024]{1,0:T(8,128)S(1)}, u32[]{:S(2)}, u32[]{:S(2)}) collective-permute-start(f32[48,1024]{1,0:T(8,128)S(1)} %slice.174), channel_id=1, source_target_pairs={{0,32},{32,0},{1,33},{33,1},{2,34},{34,2},{3,35},{35,3},{4,36},{36... | collective-permute-start | bytes 589832 | tf_op jit(solution)/shard_map/ppermute | solution.py:26
  76.5 13.9 %collective-permute-start.19 = (f32[8,128]{1,0:T(8,128)S(1)}, f32[8,128]{1,0:T(8,128)S(1)}, u32[]{:S(2)}, u32[]{:S(2)}) collective-permute-start(f32[8,128]{1,0:T(8,128)S(1)} %pad_maximum_fusion.6), channel_id=1, source_target_pairs={{0,8},{4,12},{8,16},{12,20},{16,24},{20,28},{24,0},{28,4},{1,9},{5... | collective-permute-start | bytes 12296 | tf_op jit(solution)/shard_map/ppermute | solution.py:26
  76.6 13.8 %collective-permute-start.20 = (f32[8,128]{1,0:T(8,128)S(1)}, f32[8,128]{1,0:T(8,128)S(1)}, u32[]{:S(2)}, u32[]{:S(2)}) collective-permute-start(f32[8,128]{1,0:T(8,128)S(1)} %pad_maximum_fusion.6), channel_id=1, source_target_pairs={{0,24},{4,28},{8,0},{12,4},{16,8},{20,12},{24,16},{28,20},{1,25},{... | collective-permute-start | bytes 12296 | tf_op jit(solution)/shard_map/ppermute | solution.py:26
  80.7 9.7 %collective-permute-start.21 = (f32[8,128]{1,0:T(8,128)S(1)}, f32[8,128]{1,0:T(8,128)S(1)}, u32[]{:S(2)}, u32[]{:S(2)}) collective-permute-start(f32[8,128]{1,0:T(8,128)S(1)} %pad_maximum_fusion.6), channel_id=1, source_target_pairs={{0,16},{4,20},{8,24},{12,28},{16,0},{20,4},{24,8},{28,12},{1,17},{... | collective-permute-start | bytes 12296 | tf_op jit(solution)/shard_map/ppermute | solution.py:26
  87.2 6.9 %collective-permute-start.26 = (f32[16,128]{1,0:T(8,128)S(1)}, f32[16,128]{1,0:T(8,128)S(1)}, u32[]{:S(2)}, u32[]{:S(2)}) collective-permute-start(f32[16,128]{1,0:T(8,128)S(1)} %get-tuple-element.28), channel_id=1, source_target_pairs={{0,192},{64,0},{128,64},{192,128},{1,193},{65,1},{129,65},{193,129... | collective-permute-start | bytes 24584 | tf_op jit(solution)/shard_map/ppermute | solution.py:26
  90.4 5.5 %collective-permute-start.22 = (f32[8,128]{1,0:T(8,128)S(1)}, f32[8,128]{1,0:T(8,128)S(1)}, u32[]{:S(2)}, u32[]{:S(2)}) collective-permute-start(f32[8,128]{1,0:T(8,128)S(1)} %pad_maximum_fusion.7), channel_id=1, source_target_pairs={{0,4},{4,0},{8,12},{12,8},{16,20},{20,16},{24,28},{28,24},{1,5},{5... | collective-permute-start | bytes 12296 | tf_op jit(solution)/shard_map/ppermute | solution.py:293
  90.5 5.4 %collective-permute-start.23 = (f32[8,128]{1,0:T(8,128)S(1)}, f32[8,128]{1,0:T(8,128)S(1)}, u32[]{:S(2)}, u32[]{:S(2)}) collective-permute-start(f32[8,128]{1,0:T(8,128)S(1)} %pad_maximum_fusion.7), channel_id=1, source_target_pairs={{0,2},{2,0},{1,3},{3,1},{4,6},{6,4},{5,7},{7,5},{8,10},{10,8},{9,1... | collective-permute-start | bytes 12296 | tf_op jit(solution)/shard_map/ppermute | solution.py:26
  95.6 5.2 %collective-permute-start.28 = (f32[16,128]{1,0:T(8,128)S(1)}, f32[16,128]{1,0:T(8,128)S(1)}, u32[]{:S(2)}, u32[]{:S(2)}) collective-permute-start(f32[16,128]{1,0:T(8,128)S(1)} %pad_maximum_fusion.4), channel_id=1, source_target_pairs={{0,32},{32,0},{1,33},{33,1},{2,34},{34,2},{3,35},{35,3},{4,36},{36... | collective-permute-start | bytes 24584 | tf_op jit(solution)/shard_map/ppermute | solution.py:26
  (8 other events, 122.4 us)
where the time goes:
time: 104 us
  starting transfers between devices  53.3 us (51%)
  waiting for transfers between devices  35.9 us (35%)
  Pallas kernels  11 us (11%)
  other arithmetic  2 us (2%)
  local copies, waits for them, and re-layouts  1.06 us (1%)
    ppermute x27, starting transfers between devices, shifted(): return lax.ppermute(value, axis, [(i, (i + by) % n) for i in range(n)])  51.3 us
    ppermute x27, waiting for transfers between devices, shifted(): return lax.ppermute(value, axis, [(i, (i + by) % n) for i in range(n)])  35.2 us
    pallas_call x2, Pallas kernels, tile(): pl.pallas_call(functools.partial(tile_kernel, side), out_shape=shapes, in...  5.76 us
    pallas_call x1, Pallas kernels, final(): pl.pallas_call(final_kernel, out_shape=jax.ShapeDtypeStruct((512, 1024),...  2.66 us
  transfers between devices with their start and end apart: 29, of which 12 were waited for; matrix products, arithmetic and copies ran while one was open for 3% of the time, Pallas kernels for 5%

commit v1 on v0

--- a/solution.py
+++ b/solution.py
@@ -220,21 +220,28 @@
     )(*operands)
 
 
-def final_kernel(same_ref, other_ref, inv_ref, tinv_ref, row_ref, col_ref, out_ref):
+def final_kernel(same_ref, other_ref, inv_ref, tinv_ref, row_ref, col_ref, out_ref, held, sems):
     xh = lax.axis_index("xh")
     row = from_lanes(row_ref[0:4, :] + jnp.log(row_ref[4:8, :])) - math.log(32768)
     inv = inv_ref[:, :1]
     col = col_ref[0:8, :] + jnp.log(col_ref[8:16, :]) - math.log(4096)
+    copies = []
     for side, sims_ref in enumerate((same_ref, other_ref)):
         for j in range(4):
-            place = pl.multiple_of((2 * j + (xh ^ side)) * LANES, LANES)
+            k = 4 * side + j
             right = col[4 * side + j : 4 * side + j + 1, :]
             top = jnp.maximum(row, right)
             gap = jnp.minimum(row, right) - top
             both = top + jnp.log(1.0 + jnp.exp(gap)) - math.log(2.0)
             scale = 0.5 * (inv + tinv_ref[4 * side + j : 4 * side + j + 1, :])
             sims = sims_ref[:, j * LANES : (j + 1) * LANES]
-            out_ref[:, pl.ds(place, LANES)] = sims * scale - both
+            held[k] = sims * scale - both
+            place = pl.multiple_of((2 * j + (xh ^ side)) * LANES, LANES)
+            copy = pltpu.make_async_copy(held.at[k], out_ref.at[:, pl.ds(place, LANES)], sems.at[k])
+            copy.start()
+            copies.append(copy)
+    for copy in copies:
+        copy.wait()
 
 
 def final(*operands):
@@ -242,7 +249,8 @@
         final_kernel,
         out_shape=jax.ShapeDtypeStruct((512, 1024), jnp.float32),
         in_specs=[whole()] * 6,
-        out_specs=whole(),
+        out_specs=pl.BlockSpec(memory_space=pl.ANY),
+        scratch_shapes=[pltpu.VMEM((8, 512, LANES), jnp.float32), pltpu.SemaphoreType.DMA((8,))],
         compiler_params=pltpu.CompilerParams(vmem_limit_bytes=24 << 20),
     )(*operands)
 
@@ -255,7 +263,7 @@
 
 
 def gathered_rows(own):
-    pair = jnp.stack([own, shifted(own, "xl", 1)])
+    pair = lax.optimization_barrier(jnp.stack([own, shifted(own, "xl", 1)]))
     below = shifted(pair, "z", 2)
     above = shifted(pair, "z", -2)
     across = shifted(pair, "z", 4)

time: 104 us -> 97.6 us (0.938)
  waiting for transfers between devices: 35.9 us -> 26.1 us
  starting transfers between devices: 53.3 us -> 58.7 us
    ppermute x27, waiting for transfers between devices: 35.2 us -> 26.1 us  [shifted(): return lax.ppermute(value, axis, [(i, (i + by) % n) for i in range(n)])]
    ppermute x27, starting transfers between devices: 51.3 us -> 55.5 us  [shifted(): return lax.ppermute(value, axis, [(i, (i + by) % n) for i in range(n)])]
  transfers between devices with their start and end apart: 29 -> 29, of which waited for: 12 -> 11; matrix products, arithmetic and copies ran while one was open for 3% -> 0% of each run, Pallas kernels for 5% -> 3%
where the time goes in v1:
time: 97.6 us; the launch traced here: 97.4 us
  starting transfers between devices  58.7 us (60%)
  waiting for transfers between devices  26.1 us (27%)
  Pallas kernels  10.9 us (11%)
  other arithmetic  1.15 us (1%)
    ppermute x27, starting transfers between devices, shifted(): return lax.ppermute(value, axis, [(i, (i + by) % n) for i in range(n)])  55.5 us
    ppermute x27, waiting for transfers between devices, shifted(): return lax.ppermute(value, axis, [(i, (i + by) % n) for i in range(n)])  26.1 us
    pallas_call x2, Pallas kernels, tile(): pl.pallas_call(functools.partial(tile_kernel, side), out_shape=shapes, in...  5.79 us
    pallas_call x1, Pallas kernels, final(): pl.pallas_call(final_kernel, out_shape=jax.ShapeDtypeStruct((512, 1024),...  2.58 us
    ppermute x1, starting transfers between devices, all_rows(): lax.ppermute(row, ('z', 'xl'), [(2 * i + k, 2 * (i ^ 1) + (k ^ 1)) for i...  2.19 us
    pallas_call x1, Pallas kernels, first_blocks(): pl.pallas_call(first_kernel, out_shape=(jax.ShapeDtypeStruct((144, LANES)...  1.99 us
  transfers between devices with their start and end apart: 29, of which 11 were waited for; matrix products, arithmetic and copies ran while one was open for 0% of the time, Pallas kernels for 3%

profile of v1, /device:TPU:2, one launch (start us, length us, event | category | flops | bytes accessed | tf_op | source)
XLA Modules:
  0.0 97.4 jit_solution(1286752366736017347)
XLA Ops:
  0.0 2.0 %shard_map.46 = (f32[144,128]{1,0:T(8,128)}, f32[88,1024]{1,0:T(8,128)}, f32[48,1024]{1,0:T(8,128)}) custom-call(f32[16,1024]{1,0:T(8,128)} %src_ref.1, f32[1,16]{1,0:T(1,128)} %bitcast.10, f32[128,1024]{1,0:T(8,128)} %refs_0_.1, f32[1,128]{1,0:T(1,128)} %bitcast.8), custom_call_target="tpu_custom_call" | custom-call | flops 65536 | bytes 1048576 | tf_op jit(solution)/shard_map/pallas_call | solution.py:62
  2.0 2.3 %collective-permute-start.3 = (f32[144,128]{1,0:T(8,128)}, f32[144,128]{1,0:T(8,128)S(1)}, u32[]{:S(2)}, u32[]{:S(2)}) collective-permute-start(f32[144,128]{1,0:T(8,128)} %get-tuple-element.17), channel_id=1, source_target_pairs={{0,2},{2,0},{1,3},{3,1},{4,6},{6,4},{5,7},{7,5},{8,10},{10,8},{9,1... | collective-permute-start | bytes 221192 | tf_op jit(solution)/shard_map/ppermute | solution.py:26
  4.3 2.5 %collective-permute-done.3 = f32[144,128]{1,0:T(8,128)S(1)} collective-permute-done((f32[144,128]{1,0:T(8,128)}, f32[144,128]{1,0:T(8,128)S(1)}, u32[]{:S(2)}, u32[]{:S(2)}) %collective-permute-start.3) | collective-permute-done | bytes 73760 | tf_op jit(solution)/shard_map/ppermute | solution.py:26
  7.8 3.1 %collective-permute-start.4 = (f32[2,144,128]{2,1,0:T(8,128)S(1)}, f32[2,144,128]{2,1,0:T(8,128)S(1)}, u32[]{:S(2)}, u32[]{:S(2)}) collective-permute-start(f32[2,144,128]{2,1,0:T(8,128)S(1)} %pad_maximum_fusion.4), channel_id=1, source_target_pairs={{0,8},{4,12},{8,16},{12,20},{16,24},{20,28},{24,0},{28,4},{1,9},{5... | collective-permute-start | bytes 442376 | tf_op jit(solution)/shard_map/ppermute | solution.py:26
  10.9 3.1 %collective-permute-start.5 = (f32[2,144,128]{2,1,0:T(8,128)S(1)}, f32[2,144,128]{2,1,0:T(8,128)S(1)}, u32[]{:S(2)}, u32[]{:S(2)}) collective-permute-start(f32[2,144,128]{2,1,0:T(8,128)S(1)} %pad_maximum_fusion.4), channel_id=1, source_target_pairs={{0,24},{4,28},{8,0},{12,4},{16,8},{20,12},{24,16},{28,20},{1,25},{... | collective-permute-start | bytes 442376 | tf_op jit(solution)/shard_map/ppermute | solution.py:26
  14.0 2.1 %collective-permute-start.12 = (f32[88,1024]{1,0:T(8,128)}, f32[88,1024]{1,0:T(8,128)S(1)}, u32[]{:S(2)}, u32[]{:S(2)}) collective-permute-start(f32[88,1024]{1,0:T(8,128)} %get-tuple-element.23), channel_id=1, source_target_pairs={{0,32},{32,0},{1,33},{33,1},{2,34},{34,2},{3,35},{35,3},{4,36},{36... | collective-permute-start | bytes 1081352 | tf_op jit(solution)/shard_map/ppermute | solution.py:26
  19.4 4.9 %collective-permute-start.6 = (f32[2,144,128]{2,1,0:T(8,128)S(1)}, f32[2,144,128]{2,1,0:T(8,128)S(1)}, u32[]{:S(2)}, u32[]{:S(2)}) collective-permute-start(f32[2,144,128]{2,1,0:T(8,128)S(1)} %pad_maximum_fusion.4), channel_id=1, source_target_pairs={{0,16},{4,20},{8,24},{12,28},{16,0},{20,4},{24,8},{28,12},{1,17},{... | collective-permute-start | bytes 442376 | tf_op jit(solution)/shard_map/ppermute | solution.py:26
  25.5 4.8 %collective-permute-done.6 = f32[2,144,128]{2,1,0:T(8,128)S(1)} collective-permute-done((f32[2,144,128]{2,1,0:T(8,128)S(1)}, f32[2,144,128]{2,1,0:T(8,128)S(1)}, u32[]{:S(2)}, u32[]{:S(2)}) %collective-permute-start.6) | collective-permute-done | bytes 147488 | tf_op jit(solution)/shard_map/ppermute | solution.py:26
  30.3 2.7 %collective-permute-start.2 = (f32[128,1024]{1,0:T(8,128)}, f32[128,1024]{1,0:T(8,128)S(1)}, u32[]{:S(2)}, u32[]{:S(2)}) collective-permute-start(f32[128,1024]{1,0:T(8,128)} %refs_0_.1), channel_id=1, source_target_pairs={{0,128},{64,192},{128,0},{192,64},{1,129},{65,193},{129,1},{193,65... | collective-permute-start | bytes 1572872 | tf_op jit(solution)/shard_map/ppermute | solution.py:26
  33.1 4.7 %collective-permute-start.8 = (f32[4,144,128]{2,1,0:T(8,128)S(1)}, f32[4,144,128]{2,1,0:T(8,128)S(1)}, u32[]{:S(2)}, u32[]{:S(2)}) collective-permute-start(f32[4,144,128]{2,1,0:T(8,128)S(1)} %get-tuple-element.39), channel_id=1, source_target_pairs={{0,28},{4,0},{8,4},{12,8},{16,12},{20,16},{24,20},{28,24},{1,29},{... | collective-permute-start | bytes 884744 | tf_op jit(solution)/shard_map/ppermute | solution.py:26
  38.8 2.5 %collective-permute-start.15 = (f32[88,1024]{1,0:T(8,128)S(1)}, f32[88,1024]{1,0:T(8,128)S(1)}, u32[]{:S(2)}, u32[]{:S(2)}) collective-permute-start(f32[88,1024]{1,0:T(8,128)S(1)} %select_maximum_fusion.refs_1_), channel_id=1, source_target_pairs={{0,192},{64,0},{128,64},{192,128},{1,193},{65,1},{129,65},{193,129... | collective-permute-start | bytes 1081352 | tf_op jit(solution)/shard_map/ppermute | solution.py:26
  42.1 2.2 %collective-permute-start.13 = (f32[96,1024]{1,0:T(8,128)S(1)}, f32[96,1024]{1,0:T(8,128)S(1)}, u32[]{:S(2)}, u32[]{:S(2)}) collective-permute-start(f32[96,1024]{1,0:T(8,128)S(1)} %pad_maximum_fusion.1), channel_id=1, source_target_pairs={{0,32},{32,0},{1,33},{33,1},{2,34},{34,2},{3,35},{35,3},{4,36},{36... | collective-permute-start | bytes 1179656 | tf_op jit(solution)/shard_map/ppermute | solution.py:26
  45.7 7.6 %collective-permute-done.14.refs_3_ = f32[88,1024]{1,0:T(8,128)S(1)} collective-permute-done((f32[88,1024]{1,0:T(8,128)S(1)}, f32[88,1024]{1,0:T(8,128)S(1)}, u32[]{:S(2)}, u32[]{:S(2)}) %collective-permute-start.14) | collective-permute-done | bytes 360480 | tf_op jit(solution)/shard_map/ppermute | solution.py:26
  54.4 2.2 %collective-permute-start.11 = (f32[48,1024]{1,0:T(8,128)S(1)}, f32[48,1024]{1,0:T(8,128)S(1)}, u32[]{:S(2)}, u32[]{:S(2)}) collective-permute-start(f32[48,1024]{1,0:T(8,128)S(1)} %copy-done.2), channel_id=1, source_target_pairs={{0,32},{32,0},{1,33},{33,1},{2,34},{34,2},{3,35},{35,3},{4,36},{36... | collective-permute-start | bytes 589832 | tf_op jit(solution)/shard_map/ppermute | solution.py:26
  58.4 3.5 %collective-permute-start.16 = (f32[48,1024]{1,0:T(8,128)S(1)}, f32[48,1024]{1,0:T(8,128)S(1)}, u32[]{:S(2)}, u32[]{:S(2)}) collective-permute-start(f32[48,1024]{1,0:T(8,128)S(1)} %slice.174), channel_id=1, source_target_pairs={{0,32},{32,0},{1,33},{33,1},{2,34},{34,2},{3,35},{35,3},{4,36},{36... | collective-permute-start | bytes 589832 | tf_op jit(solution)/shard_map/ppermute | solution.py:26
  62.6 2.6 %shard_map.48 = (f32[512,512]{1,0:T(8,128)S(1)}, f32[8,128]{1,0:T(8,128)S(1)}) custom-call(f32[128,1024]{1,0:T(8,128)S(1)} %copy-done, f32[128,1024]{1,0:T(8,128)S(1)} %collective-permute-done.refs_1_, f32[128,1024]{1,0:T(8,128)S(1)} %collective-permute-done.1.refs_2_, f32[128,1024]{1,0:T(8,128)S(1)} %collective-permute-done.2.refs_3_, ...), custom_call_target="tpu_custom_call" | custom-call | flops 1610612736 | bytes 6291456 | tf_op jit(solution)/shard_map/pallas_call | solution.py:210
  66.5 3.2 %shard_map.49 = (f32[512,512]{1,0:T(8,128)S(1)}, f32[8,128]{1,0:T(8,128)S(1)}, f32[16,128]{1,0:T(8,128)S(1)}, f32[8,128]{1,0:T(8,128)S(1)}) custom-call(f32[48,1024]{1,0:T(8,128)S(1)} %collective-permute-done.11.refs_0_, f32[88,1024]{1,0:T(8,128)S(1)} %select_maximum_fusion.refs_1_, f32[48,1024]{1,0:T(8,128)S(1)} %get-tuple-element.38.refs_2_, ...), custom_call_target="tpu_custom_call" | custom-call | flops 1610612736 | bytes 6291456 | tf_op jit(solution)/shard_map/pallas_call | solution.py:210
  70.9 6.4 %collective-permute-start.19 = (f32[8,128]{1,0:T(8,128)S(1)}, f32[8,128]{1,0:T(8,128)S(1)}, u32[]{:S(2)}, u32[]{:S(2)}) collective-permute-start(f32[8,128]{1,0:T(8,128)S(1)} %pad_maximum_fusion.7), channel_id=1, source_target_pairs={{0,8},{4,12},{8,16},{12,20},{16,24},{20,28},{24,0},{28,4},{1,9},{5... | collective-permute-start | bytes 12296 | tf_op jit(solution)/shard_map/ppermute | solution.py:26
  77.3 3.7 %collective-permute-start.21 = (f32[8,128]{1,0:T(8,128)S(1)}, f32[8,128]{1,0:T(8,128)S(1)}, u32[]{:S(2)}, u32[]{:S(2)}) collective-permute-start(f32[8,128]{1,0:T(8,128)S(1)} %pad_maximum_fusion.7), channel_id=1, source_target_pairs={{0,16},{4,20},{8,24},{12,28},{16,0},{20,4},{24,8},{28,12},{1,17},{... | collective-permute-start | bytes 12296 | tf_op jit(solution)/shard_map/ppermute | solution.py:26
  81.7 2.5 %collective-permute-start.26 = (f32[16,128]{1,0:T(8,128)S(1)}, f32[16,128]{1,0:T(8,128)S(1)}, u32[]{:S(2)}, u32[]{:S(2)}) collective-permute-start(f32[16,128]{1,0:T(8,128)S(1)} %get-tuple-element.28), channel_id=1, source_target_pairs={{0,192},{64,0},{128,64},{192,128},{1,193},{65,1},{129,65},{193,129... | collective-permute-start | bytes 24584 | tf_op jit(solution)/shard_map/ppermute | solution.py:26
  86.7 2.2 %collective-permute-start.24 = (f32[8,128]{1,0:T(8,128)S(1)}, f32[8,128]{1,0:T(8,128)S(1)}, u32[]{:S(2)}, u32[]{:S(2)}) collective-permute-start(f32[8,128]{1,0:T(8,128)S(1)} %pad_maximum_fusion.8), channel_id=1, source_target_pairs={{0,6},{2,4},{4,2},{6,0},{8,14},{10,12},{12,10},{14,8},{16,22},{18,... | collective-permute-start | bytes 12296 | tf_op jit(solution)/shard_map/ppermute | solution.py:302
  89.4 1.8 %collective-permute-start.28 = (f32[16,128]{1,0:T(8,128)S(1)}, f32[16,128]{1,0:T(8,128)S(1)}, u32[]{:S(2)}, u32[]{:S(2)}) collective-permute-start(f32[16,128]{1,0:T(8,128)S(1)} %pad_maximum_fusion.5), channel_id=1, source_target_pairs={{0,32},{32,0},{1,33},{33,1},{2,34},{34,2},{3,35},{35,3},{4,36},{36... | collective-permute-start | bytes 24584 | tf_op jit(solution)/shard_map/ppermute | solution.py:26
  91.3 3.4 %collective-permute-done.28 = f32[16,128]{1,0:T(8,128)S(1)} collective-permute-done((f32[16,128]{1,0:T(8,128)S(1)}, f32[16,128]{1,0:T(8,128)S(1)}, u32[]{:S(2)}, u32[]{:S(2)}) %collective-permute-start.28) | collective-permute-done | bytes 8224 | tf_op jit(solution)/shard_map/ppermute | solution.py:26
  94.7 2.6 %shard_map.50 = f32[512,1024]{1,0:T(8,128)} custom-call(f32[512,512]{1,0:T(8,128)S(1)} %get-tuple-element.21.refs_12_.same_ref, f32[512,512]{1,0:T(8,128)S(1)} %get-tuple-element.25.other_ref, f32[512,128]{1,0:T(8,128)S(1)} %get-tuple-element.20.refs_6_.refs_10_.inv_ref, f32[8,128]{1,0:T(8,128)S(1)} %get-tuple-element.26.tinv_ref, ...), custom_call_target="tpu_custom_call" | custom-call | tf_op jit(solution)/shard_map/pallas_call | solution.py:248
  (71 shorter events, 18.2 us)
Async XLA Ops:
  7.8 11.6 %collective-permute-start.4 = (f32[2,144,128]{2,1,0:T(8,128)S(1)}, f32[2,144,128]{2,1,0:T(8,128)S(1)}, u32[]{:S(2)}, u32[]{:S(2)}) collective-permute-start(f32[2,144,128]{2,1,0:T(8,128)S(1)} %pad_maximum_fusion.4), channel_id=1, source_target_pairs={{0,8},{4,12},{8,16},{12,20},{16,24},{20,28},{24,0},{28,4},{1,9},{5... | collective-permute-start | bytes 442376 | tf_op jit(solution)/shard_map/ppermute | solution.py:26
  10.9 13.4 %collective-permute-start.5 = (f32[2,144,128]{2,1,0:T(8,128)S(1)}, f32[2,144,128]{2,1,0:T(8,128)S(1)}, u32[]{:S(2)}, u32[]{:S(2)}) collective-permute-start(f32[2,144,128]{2,1,0:T(8,128)S(1)} %pad_maximum_fusion.4), channel_id=1, source_target_pairs={{0,24},{4,28},{8,0},{12,4},{16,8},{20,12},{24,16},{28,20},{1,25},{... | collective-permute-start | bytes 442376 | tf_op jit(solution)/shard_map/ppermute | solution.py:26
  14.0 19.1 %collective-permute-start.12 = (f32[88,1024]{1,0:T(8,128)}, f32[88,1024]{1,0:T(8,128)S(1)}, u32[]{:S(2)}, u32[]{:S(2)}) collective-permute-start(f32[88,1024]{1,0:T(8,128)} %get-tuple-element.23), channel_id=1, source_target_pairs={{0,32},{32,0},{1,33},{33,1},{2,34},{34,2},{3,35},{35,3},{4,36},{36... | collective-permute-start | bytes 1081352 | tf_op jit(solution)/shard_map/ppermute | solution.py:26
  16.1 22.6 %collective-permute-start = (f32[128,1024]{1,0:T(8,128)}, f32[128,1024]{1,0:T(8,128)S(1)}, u32[]{:S(2)}, u32[]{:S(2)}) collective-permute-start(f32[128,1024]{1,0:T(8,128)} %refs_0_.1), channel_id=1, source_target_pairs={{0,64},{64,128},{128,192},{192,0},{1,65},{65,129},{129,193},{193,1... | collective-permute-start | bytes 1572872 | tf_op jit(solution)/shard_map/ppermute | solution.py:26
  17.7 23.6 %collective-permute-start.1 = (f32[128,1024]{1,0:T(8,128)}, f32[128,1024]{1,0:T(8,128)S(1)}, u32[]{:S(2)}, u32[]{:S(2)}) collective-permute-start(f32[128,1024]{1,0:T(8,128)} %refs_0_.1), channel_id=1, source_target_pairs={{0,192},{64,0},{128,64},{192,128},{1,193},{65,1},{129,65},{193,129... | collective-permute-start | bytes 1572872 | tf_op jit(solution)/shard_map/ppermute | solution.py:26
  19.4 10.9 %collective-permute-start.6 = (f32[2,144,128]{2,1,0:T(8,128)S(1)}, f32[2,144,128]{2,1,0:T(8,128)S(1)}, u32[]{:S(2)}, u32[]{:S(2)}) collective-permute-start(f32[2,144,128]{2,1,0:T(8,128)S(1)} %pad_maximum_fusion.4), channel_id=1, source_target_pairs={{0,16},{4,20},{8,24},{12,28},{16,0},{20,4},{24,8},{28,12},{1,17},{... | collective-permute-start | bytes 442376 | tf_op jit(solution)/shard_map/ppermute | solution.py:26
  24.4 13.5 %collective-permute-start.7 = (f32[4,144,128]{2,1,0:T(8,128)S(1)}, f32[4,144,128]{2,1,0:T(8,128)S(1)}, u32[]{:S(2)}, u32[]{:S(2)}) collective-permute-start(f32[4,144,128]{2,1,0:T(8,128)S(1)} %get-tuple-element.40), channel_id=1, source_target_pairs={{0,4},{4,8},{8,12},{12,16},{16,20},{20,24},{24,28},{28,0},{1,5},{5... | collective-permute-start | bytes 884744 | tf_op jit(solution)/shard_map/ppermute | solution.py:26
  30.3 15.4 %collective-permute-start.2 = (f32[128,1024]{1,0:T(8,128)}, f32[128,1024]{1,0:T(8,128)S(1)}, u32[]{:S(2)}, u32[]{:S(2)}) collective-permute-start(f32[128,1024]{1,0:T(8,128)} %refs_0_.1), channel_id=1, source_target_pairs={{0,128},{64,192},{128,0},{192,64},{1,129},{65,193},{129,1},{193,65... | collective-permute-start | bytes 1572872 | tf_op jit(solution)/shard_map/ppermute | solution.py:26
  33.1 9.0 %collective-permute-start.8 = (f32[4,144,128]{2,1,0:T(8,128)S(1)}, f32[4,144,128]{2,1,0:T(8,128)S(1)}, u32[]{:S(2)}, u32[]{:S(2)}) collective-permute-start(f32[4,144,128]{2,1,0:T(8,128)S(1)} %get-tuple-element.39), channel_id=1, source_target_pairs={{0,28},{4,0},{8,4},{12,8},{16,12},{20,16},{24,20},{28,24},{1,29},{... | collective-permute-start | bytes 884744 | tf_op jit(solution)/shard_map/ppermute | solution.py:26
  37.9 15.5 %collective-permute-start.14 = (f32[88,1024]{1,0:T(8,128)S(1)}, f32[88,1024]{1,0:T(8,128)S(1)}, u32[]{:S(2)}, u32[]{:S(2)}) collective-permute-start(f32[88,1024]{1,0:T(8,128)S(1)} %select_maximum_fusion.refs_1_), channel_id=1, source_target_pairs={{0,64},{64,128},{128,192},{192,0},{1,65},{65,129},{129,193},{193,1... | collective-permute-start | bytes 1081352 | tf_op jit(solution)/shard_map/ppermute | solution.py:26
  38.8 15.6 %collective-permute-start.15 = (f32[88,1024]{1,0:T(8,128)S(1)}, f32[88,1024]{1,0:T(8,128)S(1)}, u32[]{:S(2)}, u32[]{:S(2)}) collective-permute-start(f32[88,1024]{1,0:T(8,128)S(1)} %select_maximum_fusion.refs_1_), channel_id=1, source_target_pairs={{0,192},{64,0},{128,64},{192,128},{1,193},{65,1},{129,65},{193,129... | collective-permute-start | bytes 1081352 | tf_op jit(solution)/shard_map/ppermute | solution.py:26
  41.3 17.1 %collective-permute-start.17 = (f32[88,1024]{1,0:T(8,128)S(1)}, f32[88,1024]{1,0:T(8,128)S(1)}, u32[]{:S(2)}, u32[]{:S(2)}) collective-permute-start(f32[88,1024]{1,0:T(8,128)S(1)} %select_maximum_fusion.refs_1_), channel_id=1, source_target_pairs={{0,128},{64,192},{128,0},{192,64},{1,129},{65,193},{129,1},{193,65... | collective-permute-start | bytes 1081352 | tf_op jit(solution)/shard_map/ppermute | solution.py:26
  42.1 19.9 %collective-permute-start.13 = (f32[96,1024]{1,0:T(8,128)S(1)}, f32[96,1024]{1,0:T(8,128)S(1)}, u32[]{:S(2)}, u32[]{:S(2)}) collective-permute-start(f32[96,1024]{1,0:T(8,128)S(1)} %pad_maximum_fusion.1), channel_id=1, source_target_pairs={{0,32},{32,0},{1,33},{33,1},{2,34},{34,2},{3,35},{35,3},{4,36},{36... | collective-permute-start | bytes 1179656 | tf_op jit(solution)/shard_map/ppermute | solution.py:26
  45.7 16.3 %collective-permute-start.9 = (f32[8,144,128]{2,1,0:T(8,128)S(1)}, f32[8,144,128]{2,1,0:T(8,128)S(1)}, u32[]{:S(2)}, u32[]{:S(2)}) collective-permute-start(f32[8,144,128]{2,1,0:T(8,128)S(1)} %pad_maximum_fusion.refs_0_), channel_id=1, source_target_pairs={{0,1},{1,0},{2,3},{3,2},{4,5},{5,4},{6,7},{7,6},{8,9},{9,8},{10,11... | collective-permute-start | bytes 1769480 | tf_op jit(solution)/shard_map/ppermute | solution.py:26
  53.3 8.7 %collective-permute-start.10 = (f32[8,144,128]{2,1,0:T(8,128)S(1)}, f32[8,144,128]{2,1,0:T(8,128)S(1)}, u32[]{:S(2)}, u32[]{:S(2)}) collective-permute-start(f32[8,144,128]{2,1,0:T(8,128)S(1)} %constant_dynamic-update-slice_fusion.refs_1_), channel_id=1, source_target_pairs={{0,1},{1,0},{2,3},{3,2},{4,5},{5,4},{6,7},{7,6},{8,9},{9,8},{10,11... | collective-permute-start | bytes 1769480 | tf_op jit(solution)/shard_map/ppermute | solution.py:26
  54.4 10.8 %collective-permute-start.11 = (f32[48,1024]{1,0:T(8,128)S(1)}, f32[48,1024]{1,0:T(8,128)S(1)}, u32[]{:S(2)}, u32[]{:S(2)}) collective-permute-start(f32[48,1024]{1,0:T(8,128)S(1)} %copy-done.2), channel_id=1, source_target_pairs={{0,32},{32,0},{1,33},{33,1},{2,34},{34,2},{3,35},{35,3},{4,36},{36... | collective-permute-start | bytes 589832 | tf_op jit(solution)/shard_map/ppermute | solution.py:26
  58.4 8.0 %collective-permute-start.16 = (f32[48,1024]{1,0:T(8,128)S(1)}, f32[48,1024]{1,0:T(8,128)S(1)}, u32[]{:S(2)}, u32[]{:S(2)}) collective-permute-start(f32[48,1024]{1,0:T(8,128)S(1)} %slice.174), channel_id=1, source_target_pairs={{0,32},{32,0},{1,33},{33,1},{2,34},{34,2},{3,35},{35,3},{4,36},{36... | collective-permute-start | bytes 589832 | tf_op jit(solution)/shard_map/ppermute | solution.py:26
  70.9 13.3 %collective-permute-start.19 = (f32[8,128]{1,0:T(8,128)S(1)}, f32[8,128]{1,0:T(8,128)S(1)}, u32[]{:S(2)}, u32[]{:S(2)}) collective-permute-start(f32[8,128]{1,0:T(8,128)S(1)} %pad_maximum_fusion.7), channel_id=1, source_target_pairs={{0,8},{4,12},{8,16},{12,20},{16,24},{20,28},{24,0},{28,4},{1,9},{5... | collective-permute-start | bytes 12296 | tf_op jit(solution)/shard_map/ppermute | solution.py:26
  77.3 8.0 %collective-permute-start.20 = (f32[8,128]{1,0:T(8,128)S(1)}, f32[8,128]{1,0:T(8,128)S(1)}, u32[]{:S(2)}, u32[]{:S(2)}) collective-permute-start(f32[8,128]{1,0:T(8,128)S(1)} %pad_maximum_fusion.7), channel_id=1, source_target_pairs={{0,24},{4,28},{8,0},{12,4},{16,8},{20,12},{24,16},{28,20},{1,25},{... | collective-permute-start | bytes 12296 | tf_op jit(solution)/shard_map/ppermute | solution.py:26
  77.3 8.0 %collective-permute-start.21 = (f32[8,128]{1,0:T(8,128)S(1)}, f32[8,128]{1,0:T(8,128)S(1)}, u32[]{:S(2)}, u32[]{:S(2)}) collective-permute-start(f32[8,128]{1,0:T(8,128)S(1)} %pad_maximum_fusion.7), channel_id=1, source_target_pairs={{0,16},{4,20},{8,24},{12,28},{16,0},{20,4},{24,8},{28,12},{1,17},{... | collective-permute-start | bytes 12296 | tf_op jit(solution)/shard_map/ppermute | solution.py:26
  81.0 5.8 %collective-permute-start.25 = (f32[16,128]{1,0:T(8,128)S(1)}, f32[16,128]{1,0:T(8,128)S(1)}, u32[]{:S(2)}, u32[]{:S(2)}) collective-permute-start(f32[16,128]{1,0:T(8,128)S(1)} %get-tuple-element.28), channel_id=1, source_target_pairs={{0,64},{64,128},{128,192},{192,0},{1,65},{65,129},{129,193},{193,1... | collective-permute-start | bytes 24584 | tf_op jit(solution)/shard_map/ppermute | solution.py:26
  81.7 7.2 %collective-permute-start.26 = (f32[16,128]{1,0:T(8,128)S(1)}, f32[16,128]{1,0:T(8,128)S(1)}, u32[]{:S(2)}, u32[]{:S(2)}) collective-permute-start(f32[16,128]{1,0:T(8,128)S(1)} %get-tuple-element.28), channel_id=1, source_target_pairs={{0,192},{64,0},{128,64},{192,128},{1,193},{65,1},{129,65},{193,129... | collective-permute-start | bytes 24584 | tf_op jit(solution)/shard_map/ppermute | solution.py:26
  85.4 5.9 %collective-permute-start.22 = (f32[8,128]{1,0:T(8,128)S(1)}, f32[8,128]{1,0:T(8,128)S(1)}, u32[]{:S(2)}, u32[]{:S(2)}) collective-permute-start(f32[8,128]{1,0:T(8,128)S(1)} %pad_maximum_fusion.8), channel_id=1, source_target_pairs={{0,4},{4,0},{8,12},{12,8},{16,20},{20,16},{24,28},{28,24},{1,5},{5... | collective-permute-start | bytes 12296 | tf_op jit(solution)/shard_map/ppermute | solution.py:301
  89.4 5.2 %collective-permute-start.28 = (f32[16,128]{1,0:T(8,128)S(1)}, f32[16,128]{1,0:T(8,128)S(1)}, u32[]{:S(2)}, u32[]{:S(2)}) collective-permute-start(f32[16,128]{1,0:T(8,128)S(1)} %pad_maximum_fusion.5), channel_id=1, source_target_pairs={{0,32},{32,0},{1,33},{33,1},{2,34},{34,2},{3,35},{35,3},{4,36},{36... | collective-permute-start | bytes 24584 | tf_op jit(solution)/shard_map/ppermute | solution.py:26
  (8 other events, 101.0 us)

commit v2 on v1

--- a/solution.py
+++ b/solution.py
@@ -140,21 +140,9 @@
 LAYOUTS = (((LANES,),) * 4, ((CUT, REST),) * 4)
 
 
-def tile_kernel(side, *refs):
-    n = sum(len(parts) for parts in LAYOUTS[side])
-    pieces, refs = refs[:n], refs[n:]
-    hi_ref, lo_ref, inv_ref, *refs = refs
+def split_kernel(side, *refs):
+    *pieces, bhi, blo = refs
     y = lax.axis_index("y")
-    if side == 1:
-        before_ref, before_sims, *refs = refs
-        tails, refs = refs[:4], refs[4:]
-        sims_ref, row_ref, col_ref, tinv_ref, bhi, blo = refs
-        for dy, tail in zip((0, -1, 1, 2), tails):
-            spot = lax.rem(y + dy + 4, 4)
-            tinv_ref[pl.ds(spot, 1), :] = tail[1:2, :]
-            tinv_ref[pl.ds(spot + 4, 1), :] = tail[0:1, :]
-    else:
-        sims_ref, row_ref, bhi, blo = refs
     k = 0
     for dy, parts in zip((0, -1, 1, 2), LAYOUTS[side]):
         spot = lax.rem(y + dy + 4, 4)
@@ -165,10 +153,38 @@
             total = jnp.sum(value * value, axis=1, keepdims=True)
             unit = value * lax.rsqrt(total + 1e-06)
             hi = unit.astype(jnp.bfloat16)
-            place = pl.ds(pl.multiple_of(spot * LANES + at, 8), rows)
+            place = pl.ds(pl.multiple_of(spot * LANES + at, 16), rows)
             bhi[place, :] = hi
             blo[place, :] = (unit - hi.astype(jnp.float32)).astype(jnp.bfloat16)
             at += rows
+
+
+def split(side, pieces):
+    return pl.pallas_call(
+        functools.partial(split_kernel, side),
+        out_shape=[jax.ShapeDtypeStruct((512, 1024), jnp.bfloat16)] * 2,
+        in_specs=[whole()] * len(pieces),
+        out_specs=[whole()] * 2,
+        compiler_params=pltpu.CompilerParams(vmem_limit_bytes=16 << 20),
+        cost_estimate=pl.CostEstimate(flops=4 << 20, bytes_accessed=4 << 20, transcendentals=0),
+    )(*pieces)
+
+
+def tile_kernel(side, *refs):
+    if side == 1:
+        n = sum(len(parts) for parts in LAYOUTS[side])
+        pieces, refs = refs[:n], refs[n:]
+        hi_ref, lo_ref, inv_ref, before_ref, before_sims, *refs = refs
+        tails, refs = refs[:4], refs[4:]
+        sims_ref, row_ref, col_ref, tinv_ref, bhi, blo = refs
+        y = lax.axis_index("y")
+        for dy, tail in zip((0, -1, 1, 2), tails):
+            spot = lax.rem(y + dy + 4, 4)
+            tinv_ref[pl.ds(spot, 1), :] = tail[1:2, :]
+            tinv_ref[pl.ds(spot + 4, 1), :] = tail[0:1, :]
+        split_kernel(side, *pieces, bhi, blo)
+    else:
+        bhi, blo, hi_ref, lo_ref, inv_ref, sims_ref, row_ref = refs
     dot = functools.partial(lax.dot_general, preferred_element_type=jnp.float32)
     sims = dot(hi_ref[...], bhi[...], NT)
     sims += dot(hi_ref[...], blo[...], NT)
@@ -212,7 +228,7 @@
         out_shape=shapes,
         in_specs=[whole()] * len(operands),
         out_specs=[whole()] * len(shapes),
-        scratch_shapes=[pltpu.VMEM((512, 1024), jnp.bfloat16)] * 2,
+        scratch_shapes=[pltpu.VMEM((512, 1024), jnp.bfloat16)] * (2 * side),
         compiler_params=pltpu.CompilerParams(vmem_limit_bytes=24 << 20),
         cost_estimate=pl.CostEstimate(
             flops=3 << 29, bytes_accessed=6 << 20, transcendentals=1 << 19
@@ -296,17 +312,20 @@
 
 def all_rows(row):
     row = joined([row, shifted(row, "c", 1)])
-    row = joined([row] + [shifted(row, "z", k) for k in (2, -2, 4)])
+    steps = (2, -2, 4)
+    row = joined([row] + [shifted(row, "z", k) for k in steps])
     flip = [(i, i ^ 1) for i in range(8)]
+    both = [(2 * i + k, 2 * (i ^ 1) + (k ^ 1)) for i in range(8) for k in range(2)]
     beside = lax.ppermute(row, "z", flip)
-    crossed = lax.ppermute(
-        row, ("z", "xl"), [(2 * i + k, 2 * (i ^ 1) + (k ^ 1)) for i in range(8) for k in range(2)]
-    )
-    return joined([row, beside, shifted(row, "xl", 1), crossed])
+    across = shifted(row, "xl", 1)
+    crossed = lax.ppermute(row, ("z", "xl"), both)
+    return joined([row, beside, across, crossed])
 
 
 def all_columns(col):
-    col = joined([col] + [shifted(col, "y", k) for k in (1, -1, 2)])
+    steps = (1, -1, 2)
+    parts = [shifted(col, "y", k) for k in steps]
+    col = joined([col, *parts])
     over = shifted(col, "xh", 1)
     return joined([col, jnp.concatenate([over[4:8], over[0:4], over[12:16], over[8:12]])])
 
@@ -315,6 +334,7 @@
     own, q, p = first_blocks(src, inv_src, tgt, inv_tgt)
     same, other, tails = gathered_columns(tgt, inv_tgt, q, p)
     blocks = gathered_rows(own)
+    same = split(0, same)
     hi, lo, inv = rows_ready(blocks)
     sims_same, row = tile(0, same, hi, lo, inv)
     sims_other, row, col, tinv = tile(1, other, hi, lo, inv, row, sims_same, *tails)

time: 97.6 us -> 98 us (level)
  no operation moved by 1% of the time
where the time goes in v2:
time: 98 us; the launch traced here: 97.9 us
  starting transfers between devices  58.9 us (60%)
  waiting for transfers between devices  26.5 us (27%)
  Pallas kernels  10.8 us (11%)
  other arithmetic  1.15 us (1%)
    ppermute x27, starting transfers between devices, shifted(): return lax.ppermute(value, axis, [(i, (i + by) % n) for i in range(n)])  56.1 us
    ppermute x27, waiting for transfers between devices, shifted(): return lax.ppermute(value, axis, [(i, (i + by) % n) for i in range(n)])  26.5 us
    pallas_call x2, Pallas kernels, tile(): pl.pallas_call(functools.partial(tile_kernel, side), out_shape=shapes, in...  5.19 us
    pallas_call x1, Pallas kernels, final(): pl.pallas_call(final_kernel, out_shape=jax.ShapeDtypeStruct((512, 1024),...  2.58 us
    ppermute x1, starting transfers between devices, all_rows(): crossed = lax.ppermute(row, ('z', 'xl'), both)  2.17 us
    pallas_call x1, Pallas kernels, first_blocks(): pl.pallas_call(first_kernel, out_shape=(jax.ShapeDtypeStruct((144, LANES)...  2 us
  transfers between devices with their start and end apart: 29, of which 11 were waited for; matrix products, arithmetic and copies ran while one was open for 0% of the time, Pallas kernels for 3%

profile of v2, /device:TPU:2, one launch (start us, length us, event | category | flops | bytes accessed | tf_op | source)
XLA Modules:
  0.0 97.9 jit_solution(16924001504359931258)
XLA Ops:
  0.0 2.0 %shard_map.47 = (f32[144,128]{1,0:T(8,128)}, f32[88,1024]{1,0:T(8,128)}, f32[48,1024]{1,0:T(8,128)}) custom-call(f32[16,1024]{1,0:T(8,128)} %src_ref.1, f32[1,16]{1,0:T(1,128)} %bitcast.10, f32[128,1024]{1,0:T(8,128)} %tgt_ref.1, f32[1,128]{1,0:T(1,128)} %bitcast.8), custom_call_target="tpu_custom_call" | custom-call | flops 65536 | bytes 1048576 | tf_op jit(solution)/shard_map/pallas_call | solution.py:62
  2.0 2.3 %collective-permute-start.3 = (f32[144,128]{1,0:T(8,128)}, f32[144,128]{1,0:T(8,128)S(1)}, u32[]{:S(2)}, u32[]{:S(2)}) collective-permute-start(f32[144,128]{1,0:T(8,128)} %get-tuple-element.21), channel_id=1, source_target_pairs={{0,2},{2,0},{1,3},{3,1},{4,6},{6,4},{5,7},{7,5},{8,10},{10,8},{9,1... | collective-permute-start | bytes 221192 | tf_op jit(solution)/shard_map/ppermute | solution.py:26
  4.3 2.5 %collective-permute-done.3 = f32[144,128]{1,0:T(8,128)S(1)} collective-permute-done((f32[144,128]{1,0:T(8,128)}, f32[144,128]{1,0:T(8,128)S(1)}, u32[]{:S(2)}, u32[]{:S(2)}) %collective-permute-start.3) | collective-permute-done | bytes 73760 | tf_op jit(solution)/shard_map/ppermute | solution.py:26
  7.8 3.1 %collective-permute-start.4 = (f32[2,144,128]{2,1,0:T(8,128)S(1)}, f32[2,144,128]{2,1,0:T(8,128)S(1)}, u32[]{:S(2)}, u32[]{:S(2)}) collective-permute-start(f32[2,144,128]{2,1,0:T(8,128)S(1)} %pad_maximum_fusion.4), channel_id=1, source_target_pairs={{0,8},{4,12},{8,16},{12,20},{16,24},{20,28},{24,0},{28,4},{1,9},{5... | collective-permute-start | bytes 442376 | tf_op jit(solution)/shard_map/ppermute | solution.py:26
  10.9 3.1 %collective-permute-start.5 = (f32[2,144,128]{2,1,0:T(8,128)S(1)}, f32[2,144,128]{2,1,0:T(8,128)S(1)}, u32[]{:S(2)}, u32[]{:S(2)}) collective-permute-start(f32[2,144,128]{2,1,0:T(8,128)S(1)} %pad_maximum_fusion.4), channel_id=1, source_target_pairs={{0,24},{4,28},{8,0},{12,4},{16,8},{20,12},{24,16},{28,20},{1,25},{... | collective-permute-start | bytes 442376 | tf_op jit(solution)/shard_map/ppermute | solution.py:26
  14.0 2.1 %collective-permute-start.12 = (f32[88,1024]{1,0:T(8,128)}, f32[88,1024]{1,0:T(8,128)S(1)}, u32[]{:S(2)}, u32[]{:S(2)}) collective-permute-start(f32[88,1024]{1,0:T(8,128)} %get-tuple-element.27), channel_id=1, source_target_pairs={{0,32},{32,0},{1,33},{33,1},{2,34},{34,2},{3,35},{35,3},{4,36},{36... | collective-permute-start | bytes 1081352 | tf_op jit(solution)/shard_map/ppermute | solution.py:26
  19.4 4.9 %collective-permute-start.6 = (f32[2,144,128]{2,1,0:T(8,128)S(1)}, f32[2,144,128]{2,1,0:T(8,128)S(1)}, u32[]{:S(2)}, u32[]{:S(2)}) collective-permute-start(f32[2,144,128]{2,1,0:T(8,128)S(1)} %pad_maximum_fusion.4), channel_id=1, source_target_pairs={{0,16},{4,20},{8,24},{12,28},{16,0},{20,4},{24,8},{28,12},{1,17},{... | collective-permute-start | bytes 442376 | tf_op jit(solution)/shard_map/ppermute | solution.py:26
  25.5 4.8 %collective-permute-done.6 = f32[2,144,128]{2,1,0:T(8,128)S(1)} collective-permute-done((f32[2,144,128]{2,1,0:T(8,128)S(1)}, f32[2,144,128]{2,1,0:T(8,128)S(1)}, u32[]{:S(2)}, u32[]{:S(2)}) %collective-permute-start.6) | collective-permute-done | bytes 147488 | tf_op jit(solution)/shard_map/ppermute | solution.py:26
  30.3 2.7 %collective-permute-start.2 = (f32[128,1024]{1,0:T(8,128)}, f32[128,1024]{1,0:T(8,128)S(1)}, u32[]{:S(2)}, u32[]{:S(2)}) collective-permute-start(f32[128,1024]{1,0:T(8,128)} %tgt_ref.1), channel_id=1, source_target_pairs={{0,128},{64,192},{128,0},{192,64},{1,129},{65,193},{129,1},{193,65... | collective-permute-start | bytes 1572872 | tf_op jit(solution)/shard_map/ppermute | solution.py:26
  33.1 4.7 %collective-permute-start.8 = (f32[4,144,128]{2,1,0:T(8,128)S(1)}, f32[4,144,128]{2,1,0:T(8,128)S(1)}, u32[]{:S(2)}, u32[]{:S(2)}) collective-permute-start(f32[4,144,128]{2,1,0:T(8,128)S(1)} %get-tuple-element.43), channel_id=1, source_target_pairs={{0,28},{4,0},{8,4},{12,8},{16,12},{20,16},{24,20},{28,24},{1,29},{... | collective-permute-start | bytes 884744 | tf_op jit(solution)/shard_map/ppermute | solution.py:26
  38.8 2.5 %collective-permute-start.15 = (f32[88,1024]{1,0:T(8,128)S(1)}, f32[88,1024]{1,0:T(8,128)S(1)}, u32[]{:S(2)}, u32[]{:S(2)}) collective-permute-start(f32[88,1024]{1,0:T(8,128)S(1)} %select_maximum_fusion.refs_1_), channel_id=1, source_target_pairs={{0,192},{64,0},{128,64},{192,128},{1,193},{65,1},{129,65},{193,129... | collective-permute-start | bytes 1081352 | tf_op jit(solution)/shard_map/ppermute | solution.py:26
  42.1 2.2 %collective-permute-start.13 = (f32[96,1024]{1,0:T(8,128)S(1)}, f32[96,1024]{1,0:T(8,128)S(1)}, u32[]{:S(2)}, u32[]{:S(2)}) collective-permute-start(f32[96,1024]{1,0:T(8,128)S(1)} %pad_maximum_fusion.1), channel_id=1, source_target_pairs={{0,32},{32,0},{1,33},{33,1},{2,34},{34,2},{3,35},{35,3},{4,36},{36... | collective-permute-start | bytes 1179656 | tf_op jit(solution)/shard_map/ppermute | solution.py:26
  45.7 7.6 %collective-permute-done.14.refs_3_ = f32[88,1024]{1,0:T(8,128)S(1)} collective-permute-done((f32[88,1024]{1,0:T(8,128)S(1)}, f32[88,1024]{1,0:T(8,128)S(1)}, u32[]{:S(2)}, u32[]{:S(2)}) %collective-permute-start.14) | collective-permute-done | bytes 360480 | tf_op jit(solution)/shard_map/ppermute | solution.py:26
  54.4 2.4 %collective-permute-start.11 = (f32[48,1024]{1,0:T(8,128)S(1)}, f32[48,1024]{1,0:T(8,128)S(1)}, u32[]{:S(2)}, u32[]{:S(2)}) collective-permute-start(f32[48,1024]{1,0:T(8,128)S(1)} %copy-done.2), channel_id=1, source_target_pairs={{0,32},{32,0},{1,33},{33,1},{2,34},{34,2},{3,35},{35,3},{4,36},{36... | collective-permute-start | bytes 589832 | tf_op jit(solution)/shard_map/ppermute | solution.py:26
  58.5 3.5 %collective-permute-start.16 = (f32[48,1024]{1,0:T(8,128)S(1)}, f32[48,1024]{1,0:T(8,128)S(1)}, u32[]{:S(2)}, u32[]{:S(2)}) collective-permute-start(f32[48,1024]{1,0:T(8,128)S(1)} %slice.174), channel_id=1, source_target_pairs={{0,32},{32,0},{1,33},{33,1},{2,34},{34,2},{3,35},{35,3},{4,36},{36... | collective-permute-start | bytes 589832 | tf_op jit(solution)/shard_map/ppermute | solution.py:26
  62.6 2.0 %shard_map.49 = (f32[512,512]{1,0:T(8,128)S(1)}, f32[8,128]{1,0:T(8,128)S(1)}) custom-call(bf16[512,1024]{1,0:T(8,128)(2,1)S(1)} %get-tuple-element.19.refs_0_, bf16[512,1024]{1,0:T(8,128)(2,1)S(1)} %get-tuple-element.20.refs_1_, bf16[512,1024]{1,0:T(8,128)(2,1)S(1)} %get-tuple-element.22.refs_2_.refs_8_, ...), custom_call_target="tpu_custom_call" | custom-call | flops 1610612736 | bytes 6291456 | tf_op jit(solution)/shard_map/pallas_call | solution.py:226
  64.7 2.3 %collective-permute-done.16.refs_6_ = f32[48,1024]{1,0:T(8,128)S(1)} collective-permute-done((f32[48,1024]{1,0:T(8,128)S(1)}, f32[48,1024]{1,0:T(8,128)S(1)}, u32[]{:S(2)}, u32[]{:S(2)}) %collective-permute-start.16) | collective-permute-done | bytes 196640 | tf_op jit(solution)/shard_map/ppermute | solution.py:26
  67.0 3.1 %shard_map.50 = (f32[512,512]{1,0:T(8,128)S(1)}, f32[8,128]{1,0:T(8,128)S(1)}, f32[16,128]{1,0:T(8,128)S(1)}, f32[8,128]{1,0:T(8,128)S(1)}) custom-call(f32[48,1024]{1,0:T(8,128)S(1)} %collective-permute-done.11.refs_0_, f32[88,1024]{1,0:T(8,128)S(1)} %select_maximum_fusion.refs_1_, f32[48,1024]{1,0:T(8,128)S(1)} %get-tuple-element.42.refs_2_, ...), custom_call_target="tpu_custom_call" | custom-call | flops 1610612736 | bytes 6291456 | tf_op jit(solution)/shard_map/pallas_call | solution.py:226
  71.4 6.4 %collective-permute-start.19 = (f32[8,128]{1,0:T(8,128)S(1)}, f32[8,128]{1,0:T(8,128)S(1)}, u32[]{:S(2)}, u32[]{:S(2)}) collective-permute-start(f32[8,128]{1,0:T(8,128)S(1)} %pad_maximum_fusion.7), channel_id=1, source_target_pairs={{0,8},{4,12},{8,16},{12,20},{16,24},{20,28},{24,0},{28,4},{1,9},{5... | collective-permute-start | bytes 12296 | tf_op jit(solution)/shard_map/ppermute | solution.py:26
  77.8 3.7 %collective-permute-start.21 = (f32[8,128]{1,0:T(8,128)S(1)}, f32[8,128]{1,0:T(8,128)S(1)}, u32[]{:S(2)}, u32[]{:S(2)}) collective-permute-start(f32[8,128]{1,0:T(8,128)S(1)} %pad_maximum_fusion.7), channel_id=1, source_target_pairs={{0,16},{4,20},{8,24},{12,28},{16,0},{20,4},{24,8},{28,12},{1,17},{... | collective-permute-start | bytes 12296 | tf_op jit(solution)/shard_map/ppermute | solution.py:26
  82.2 2.5 %collective-permute-start.26 = (f32[16,128]{1,0:T(8,128)S(1)}, f32[16,128]{1,0:T(8,128)S(1)}, u32[]{:S(2)}, u32[]{:S(2)}) collective-permute-start(f32[16,128]{1,0:T(8,128)S(1)} %get-tuple-element.32), channel_id=1, source_target_pairs={{0,192},{64,0},{128,64},{192,128},{1,193},{65,1},{129,65},{193,129... | collective-permute-start | bytes 24584 | tf_op jit(solution)/shard_map/ppermute | solution.py:26
  87.2 2.2 %collective-permute-start.24 = (f32[8,128]{1,0:T(8,128)S(1)}, f32[8,128]{1,0:T(8,128)S(1)}, u32[]{:S(2)}, u32[]{:S(2)}) collective-permute-start(f32[8,128]{1,0:T(8,128)S(1)} %pad_maximum_fusion.8), channel_id=1, source_target_pairs={{0,6},{2,4},{4,2},{6,0},{8,14},{10,12},{12,10},{14,8},{16,22},{18,... | collective-permute-start | bytes 12296 | tf_op jit(solution)/shard_map/ppermute | solution.py:321
  91.8 3.4 %collective-permute-done.28 = f32[16,128]{1,0:T(8,128)S(1)} collective-permute-done((f32[16,128]{1,0:T(8,128)S(1)}, f32[16,128]{1,0:T(8,128)S(1)}, u32[]{:S(2)}, u32[]{:S(2)}) %collective-permute-start.28) | collective-permute-done | bytes 8224 | tf_op jit(solution)/shard_map/ppermute | solution.py:26
  95.2 2.6 %shard_map.51 = f32[512,1024]{1,0:T(8,128)} custom-call(f32[512,512]{1,0:T(8,128)S(1)} %get-tuple-element.25.refs_12_.same_ref, f32[512,512]{1,0:T(8,128)S(1)} %get-tuple-element.29.other_ref, f32[512,128]{1,0:T(8,128)S(1)} %get-tuple-element.24.refs_4_.refs_10_.inv_ref, f32[8,128]{1,0:T(8,128)S(1)} %get-tuple-element.30.tinv_ref, ...), custom_call_target="tpu_custom_call" | custom-call | tf_op jit(solution)/shard_map/pallas_call | solution.py:264
  (72 shorter events, 18.6 us)
Async XLA Ops:
  7.8 11.6 %collective-permute-start.4 = (f32[2,144,128]{2,1,0:T(8,128)S(1)}, f32[2,144,128]{2,1,0:T(8,128)S(1)}, u32[]{:S(2)}, u32[]{:S(2)}) collective-permute-start(f32[2,144,128]{2,1,0:T(8,128)S(1)} %pad_maximum_fusion.4), channel_id=1, source_target_pairs={{0,8},{4,12},{8,16},{12,20},{16,24},{20,28},{24,0},{28,4},{1,9},{5... | collective-permute-start | bytes 442376 | tf_op jit(solution)/shard_map/ppermute | solution.py:26
  10.9 13.4 %collective-permute-start.5 = (f32[2,144,128]{2,1,0:T(8,128)S(1)}, f32[2,144,128]{2,1,0:T(8,128)S(1)}, u32[]{:S(2)}, u32[]{:S(2)}) collective-permute-start(f32[2,144,128]{2,1,0:T(8,128)S(1)} %pad_maximum_fusion.4), channel_id=1, source_target_pairs={{0,24},{4,28},{8,0},{12,4},{16,8},{20,12},{24,16},{28,20},{1,25},{... | collective-permute-start | bytes 442376 | tf_op jit(solution)/shard_map/ppermute | solution.py:26
  14.0 19.1 %collective-permute-start.12 = (f32[88,1024]{1,0:T(8,128)}, f32[88,1024]{1,0:T(8,128)S(1)}, u32[]{:S(2)}, u32[]{:S(2)}) collective-permute-start(f32[88,1024]{1,0:T(8,128)} %get-tuple-element.27), channel_id=1, source_target_pairs={{0,32},{32,0},{1,33},{33,1},{2,34},{34,2},{3,35},{35,3},{4,36},{36... | collective-permute-start | bytes 1081352 | tf_op jit(solution)/shard_map/ppermute | solution.py:26
  16.2 22.6 %collective-permute-start = (f32[128,1024]{1,0:T(8,128)}, f32[128,1024]{1,0:T(8,128)S(1)}, u32[]{:S(2)}, u32[]{:S(2)}) collective-permute-start(f32[128,1024]{1,0:T(8,128)} %tgt_ref.1), channel_id=1, source_target_pairs={{0,64},{64,128},{128,192},{192,0},{1,65},{65,129},{129,193},{193,1... | collective-permute-start | bytes 1572872 | tf_op jit(solution)/shard_map/ppermute | solution.py:26
  17.7 23.6 %collective-permute-start.1 = (f32[128,1024]{1,0:T(8,128)}, f32[128,1024]{1,0:T(8,128)S(1)}, u32[]{:S(2)}, u32[]{:S(2)}) collective-permute-start(f32[128,1024]{1,0:T(8,128)} %tgt_ref.1), channel_id=1, source_target_pairs={{0,192},{64,0},{128,64},{192,128},{1,193},{65,1},{129,65},{193,129... | collective-permute-start | bytes 1572872 | tf_op jit(solution)/shard_map/ppermute | solution.py:26
  19.4 10.9 %collective-permute-start.6 = (f32[2,144,128]{2,1,0:T(8,128)S(1)}, f32[2,144,128]{2,1,0:T(8,128)S(1)}, u32[]{:S(2)}, u32[]{:S(2)}) collective-permute-start(f32[2,144,128]{2,1,0:T(8,128)S(1)} %pad_maximum_fusion.4), channel_id=1, source_target_pairs={{0,16},{4,20},{8,24},{12,28},{16,0},{20,4},{24,8},{28,12},{1,17},{... | collective-permute-start | bytes 442376 | tf_op jit(solution)/shard_map/ppermute | solution.py:26
  24.4 13.5 %collective-permute-start.7 = (f32[4,144,128]{2,1,0:T(8,128)S(1)}, f32[4,144,128]{2,1,0:T(8,128)S(1)}, u32[]{:S(2)}, u32[]{:S(2)}) collective-permute-start(f32[4,144,128]{2,1,0:T(8,128)S(1)} %get-tuple-element.44), channel_id=1, source_target_pairs={{0,4},{4,8},{8,12},{12,16},{16,20},{20,24},{24,28},{28,0},{1,5},{5... | collective-permute-start | bytes 884744 | tf_op jit(solution)/shard_map/ppermute | solution.py:26
  30.3 15.4 %collective-permute-start.2 = (f32[128,1024]{1,0:T(8,128)}, f32[128,1024]{1,0:T(8,128)S(1)}, u32[]{:S(2)}, u32[]{:S(2)}) collective-permute-start(f32[128,1024]{1,0:T(8,128)} %tgt_ref.1), channel_id=1, source_target_pairs={{0,128},{64,192},{128,0},{192,64},{1,129},{65,193},{129,1},{193,65... | collective-permute-start | bytes 1572872 | tf_op jit(solution)/shard_map/ppermute | solution.py:26
  33.1 9.0 %collective-permute-start.8 = (f32[4,144,128]{2,1,0:T(8,128)S(1)}, f32[4,144,128]{2,1,0:T(8,128)S(1)}, u32[]{:S(2)}, u32[]{:S(2)}) collective-permute-start(f32[4,144,128]{2,1,0:T(8,128)S(1)} %get-tuple-element.43), channel_id=1, source_target_pairs={{0,28},{4,0},{8,4},{12,8},{16,12},{20,16},{24,20},{28,24},{1,29},{... | collective-permute-start | bytes 884744 | tf_op jit(solution)/shard_map/ppermute | solution.py:26
  37.9 15.4 %collective-permute-start.14 = (f32[88,1024]{1,0:T(8,128)S(1)}, f32[88,1024]{1,0:T(8,128)S(1)}, u32[]{:S(2)}, u32[]{:S(2)}) collective-permute-start(f32[88,1024]{1,0:T(8,128)S(1)} %select_maximum_fusion.refs_1_), channel_id=1, source_target_pairs={{0,64},{64,128},{128,192},{192,0},{1,65},{65,129},{129,193},{193,1... | collective-permute-start | bytes 1081352 | tf_op jit(solution)/shard_map/ppermute | solution.py:26
  38.8 15.6 %collective-permute-start.15 = (f32[88,1024]{1,0:T(8,128)S(1)}, f32[88,1024]{1,0:T(8,128)S(1)}, u32[]{:S(2)}, u32[]{:S(2)}) collective-permute-start(f32[88,1024]{1,0:T(8,128)S(1)} %select_maximum_fusion.refs_1_), channel_id=1, source_target_pairs={{0,192},{64,0},{128,64},{192,128},{1,193},{65,1},{129,65},{193,129... | collective-permute-start | bytes 1081352 | tf_op jit(solution)/shard_map/ppermute | solution.py:26
  41.3 17.1 %collective-permute-start.17 = (f32[88,1024]{1,0:T(8,128)S(1)}, f32[88,1024]{1,0:T(8,128)S(1)}, u32[]{:S(2)}, u32[]{:S(2)}) collective-permute-start(f32[88,1024]{1,0:T(8,128)S(1)} %select_maximum_fusion.refs_1_), channel_id=1, source_target_pairs={{0,128},{64,192},{128,0},{192,64},{1,129},{65,193},{129,1},{193,65... | collective-permute-start | bytes 1081352 | tf_op jit(solution)/shard_map/ppermute | solution.py:26
  42.1 19.9 %collective-permute-start.13 = (f32[96,1024]{1,0:T(8,128)S(1)}, f32[96,1024]{1,0:T(8,128)S(1)}, u32[]{:S(2)}, u32[]{:S(2)}) collective-permute-start(f32[96,1024]{1,0:T(8,128)S(1)} %pad_maximum_fusion.1), channel_id=1, source_target_pairs={{0,32},{32,0},{1,33},{33,1},{2,34},{34,2},{3,35},{35,3},{4,36},{36... | collective-permute-start | bytes 1179656 | tf_op jit(solution)/shard_map/ppermute | solution.py:26
  45.7 16.3 %collective-permute-start.9 = (f32[8,144,128]{2,1,0:T(8,128)S(1)}, f32[8,144,128]{2,1,0:T(8,128)S(1)}, u32[]{:S(2)}, u32[]{:S(2)}) collective-permute-start(f32[8,144,128]{2,1,0:T(8,128)S(1)} %pad_maximum_fusion.refs_0_), channel_id=1, source_target_pairs={{0,1},{1,0},{2,3},{3,2},{4,5},{5,4},{6,7},{7,6},{8,9},{9,8},{10,11... | collective-permute-start | bytes 1769480 | tf_op jit(solution)/shard_map/ppermute | solution.py:26
  53.3 8.7 %collective-permute-start.10 = (f32[8,144,128]{2,1,0:T(8,128)S(1)}, f32[8,144,128]{2,1,0:T(8,128)S(1)}, u32[]{:S(2)}, u32[]{:S(2)}) collective-permute-start(f32[8,144,128]{2,1,0:T(8,128)S(1)} %constant_dynamic-update-slice_fusion.refs_1_), channel_id=1, source_target_pairs={{0,1},{1,0},{2,3},{3,2},{4,5},{5,4},{6,7},{7,6},{8,9},{9,8},{10,11... | collective-permute-start | bytes 1769480 | tf_op jit(solution)/shard_map/ppermute | solution.py:26
  54.4 10.2 %collective-permute-start.11 = (f32[48,1024]{1,0:T(8,128)S(1)}, f32[48,1024]{1,0:T(8,128)S(1)}, u32[]{:S(2)}, u32[]{:S(2)}) collective-permute-start(f32[48,1024]{1,0:T(8,128)S(1)} %copy-done.2), channel_id=1, source_target_pairs={{0,32},{32,0},{1,33},{33,1},{2,34},{34,2},{3,35},{35,3},{4,36},{36... | collective-permute-start | bytes 589832 | tf_op jit(solution)/shard_map/ppermute | solution.py:26
  58.5 8.5 %collective-permute-start.16 = (f32[48,1024]{1,0:T(8,128)S(1)}, f32[48,1024]{1,0:T(8,128)S(1)}, u32[]{:S(2)}, u32[]{:S(2)}) collective-permute-start(f32[48,1024]{1,0:T(8,128)S(1)} %slice.174), channel_id=1, source_target_pairs={{0,32},{32,0},{1,33},{33,1},{2,34},{34,2},{3,35},{35,3},{4,36},{36... | collective-permute-start | bytes 589832 | tf_op jit(solution)/shard_map/ppermute | solution.py:26
  71.4 13.3 %collective-permute-start.19 = (f32[8,128]{1,0:T(8,128)S(1)}, f32[8,128]{1,0:T(8,128)S(1)}, u32[]{:S(2)}, u32[]{:S(2)}) collective-permute-start(f32[8,128]{1,0:T(8,128)S(1)} %pad_maximum_fusion.7), channel_id=1, source_target_pairs={{0,8},{4,12},{8,16},{12,20},{16,24},{20,28},{24,0},{28,4},{1,9},{5... | collective-permute-start | bytes 12296 | tf_op jit(solution)/shard_map/ppermute | solution.py:26
  77.8 8.0 %collective-permute-start.20 = (f32[8,128]{1,0:T(8,128)S(1)}, f32[8,128]{1,0:T(8,128)S(1)}, u32[]{:S(2)}, u32[]{:S(2)}) collective-permute-start(f32[8,128]{1,0:T(8,128)S(1)} %pad_maximum_fusion.7), channel_id=1, source_target_pairs={{0,24},{4,28},{8,0},{12,4},{16,8},{20,12},{24,16},{28,20},{1,25},{... | collective-permute-start | bytes 12296 | tf_op jit(solution)/shard_map/ppermute | solution.py:26
  77.8 8.0 %collective-permute-start.21 = (f32[8,128]{1,0:T(8,128)S(1)}, f32[8,128]{1,0:T(8,128)S(1)}, u32[]{:S(2)}, u32[]{:S(2)}) collective-permute-start(f32[8,128]{1,0:T(8,128)S(1)} %pad_maximum_fusion.7), channel_id=1, source_target_pairs={{0,16},{4,20},{8,24},{12,28},{16,0},{20,4},{24,8},{28,12},{1,17},{... | collective-permute-start | bytes 12296 | tf_op jit(solution)/shard_map/ppermute | solution.py:26
  81.5 5.8 %collective-permute-start.25 = (f32[16,128]{1,0:T(8,128)S(1)}, f32[16,128]{1,0:T(8,128)S(1)}, u32[]{:S(2)}, u32[]{:S(2)}) collective-permute-start(f32[16,128]{1,0:T(8,128)S(1)} %get-tuple-element.32), channel_id=1, source_target_pairs={{0,64},{64,128},{128,192},{192,0},{1,65},{65,129},{129,193},{193,1... | collective-permute-start | bytes 24584 | tf_op jit(solution)/shard_map/ppermute | solution.py:26
  82.2 7.2 %collective-permute-start.26 = (f32[16,128]{1,0:T(8,128)S(1)}, f32[16,128]{1,0:T(8,128)S(1)}, u32[]{:S(2)}, u32[]{:S(2)}) collective-permute-start(f32[16,128]{1,0:T(8,128)S(1)} %get-tuple-element.32), channel_id=1, source_target_pairs={{0,192},{64,0},{128,64},{192,128},{1,193},{65,1},{129,65},{193,129... | collective-permute-start | bytes 24584 | tf_op jit(solution)/shard_map/ppermute | solution.py:26
  85.8 5.9 %collective-permute-start.22 = (f32[8,128]{1,0:T(8,128)S(1)}, f32[8,128]{1,0:T(8,128)S(1)}, u32[]{:S(2)}, u32[]{:S(2)}) collective-permute-start(f32[8,128]{1,0:T(8,128)S(1)} %pad_maximum_fusion.8), channel_id=1, source_target_pairs={{0,4},{4,0},{8,12},{12,8},{16,20},{20,16},{24,28},{28,24},{1,5},{5... | collective-permute-start | bytes 12296 | tf_op jit(solution)/shard_map/ppermute | solution.py:319
  86.4 5.3 %collective-permute-start.23 = (f32[8,128]{1,0:T(8,128)S(1)}, f32[8,128]{1,0:T(8,128)S(1)}, u32[]{:S(2)}, u32[]{:S(2)}) collective-permute-start(f32[8,128]{1,0:T(8,128)S(1)} %pad_maximum_fusion.8), channel_id=1, source_target_pairs={{0,2},{2,0},{1,3},{3,1},{4,6},{6,4},{5,7},{7,5},{8,10},{10,8},{9,1... | collective-permute-start | bytes 12296 | tf_op jit(solution)/shard_map/ppermute | solution.py:26
  (8 other events, 92.2 us)

commit v3 on v2

--- a/solution.py
+++ b/solution.py
@@ -312,20 +312,17 @@
 
 def all_rows(row):
     row = joined([row, shifted(row, "c", 1)])
-    steps = (2, -2, 4)
-    row = joined([row] + [shifted(row, "z", k) for k in steps])
+    row = joined([row] + [shifted(row, "z", k) for k in (2, -2, 4)])
     flip = [(i, i ^ 1) for i in range(8)]
-    both = [(2 * i + k, 2 * (i ^ 1) + (k ^ 1)) for i in range(8) for k in range(2)]
     beside = lax.ppermute(row, "z", flip)
-    across = shifted(row, "xl", 1)
-    crossed = lax.ppermute(row, ("z", "xl"), both)
-    return joined([row, beside, across, crossed])
+    crossed = lax.ppermute(
+        row, ("z", "xl"), [(2 * i + k, 2 * (i ^ 1) + (k ^ 1)) for i in range(8) for k in range(2)]
+    )
+    return joined([row, beside, shifted(row, "xl", 1), crossed])
 
 
 def all_columns(col):
-    steps = (1, -1, 2)
-    parts = [shifted(col, "y", k) for k in steps]
-    col = joined([col, *parts])
+    col = joined([col] + [shifted(col, "y", k) for k in (1, -1, 2)])
     over = shifted(col, "xh", 1)
     return joined([col, jnp.concatenate([over[4:8], over[0:4], over[12:16], over[8:12]])])
 

time: 98 us -> 98 us (level)
  no operation moved by 1% of the time
where the time goes in v3:
time: 98 us; the launch traced here: 97.9 us
  starting transfers between devices  58.9 us (60%)
  waiting for transfers between devices  26.5 us (27%)
  Pallas kernels  10.8 us (11%)
  other arithmetic  1.15 us (1%)
    ppermute x27, starting transfers between devices, shifted(): return lax.ppermute(value, axis, [(i, (i + by) % n) for i in range(n)])  56.1 us
    ppermute x27, waiting for transfers between devices, shifted(): return lax.ppermute(value, axis, [(i, (i + by) % n) for i in range(n)])  26.5 us
    pallas_call x2, Pallas kernels, tile(): pl.pallas_call(functools.partial(tile_kernel, side), out_shape=shapes, in...  5.19 us
    pallas_call x1, Pallas kernels, final(): pl.pallas_call(final_kernel, out_shape=jax.ShapeDtypeStruct((512, 1024),...  2.58 us
    ppermute x1, starting transfers between devices, all_rows(): lax.ppermute(row, ('z', 'xl'), [(2 * i + k, 2 * (i ^ 1) + (k ^ 1)) for i...  2.17 us
    pallas_call x1, Pallas kernels, first_blocks(): pl.pallas_call(first_kernel, out_shape=(jax.ShapeDtypeStruct((144, LANES)...  2 us
  transfers between devices with their start and end apart: 29, of which 11 were waited for; matrix products, arithmetic and copies ran while one was open for 0% of the time, Pallas kernels for 3%

profile of v3, /device:TPU:2, one launch (start us, length us, event | category | flops | bytes accessed | tf_op | source)
XLA Modules:
  0.0 97.9 jit_solution(16924001504359931258)
XLA Ops:
  0.0 2.0 %shard_map.47 = (f32[144,128]{1,0:T(8,128)}, f32[88,1024]{1,0:T(8,128)}, f32[48,1024]{1,0:T(8,128)}) custom-call(f32[16,1024]{1,0:T(8,128)} %src_ref.1, f32[1,16]{1,0:T(1,128)} %bitcast.10, f32[128,1024]{1,0:T(8,128)} %tgt_ref.1, f32[1,128]{1,0:T(1,128)} %bitcast.8), custom_call_target="tpu_custom_call" | custom-call | flops 65536 | bytes 1048576 | tf_op jit(solution)/shard_map/pallas_call | solution.py:62
  2.0 2.3 %collective-permute-start.3 = (f32[144,128]{1,0:T(8,128)}, f32[144,128]{1,0:T(8,128)S(1)}, u32[]{:S(2)}, u32[]{:S(2)}) collective-permute-start(f32[144,128]{1,0:T(8,128)} %get-tuple-element.21), channel_id=1, source_target_pairs={{0,2},{2,0},{1,3},{3,1},{4,6},{6,4},{5,7},{7,5},{8,10},{10,8},{9,1... | collective-permute-start | bytes 221192 | tf_op jit(solution)/shard_map/ppermute | solution.py:26
  4.3 2.5 %collective-permute-done.3 = f32[144,128]{1,0:T(8,128)S(1)} collective-permute-done((f32[144,128]{1,0:T(8,128)}, f32[144,128]{1,0:T(8,128)S(1)}, u32[]{:S(2)}, u32[]{:S(2)}) %collective-permute-start.3) | collective-permute-done | bytes 73760 | tf_op jit(solution)/shard_map/ppermute | solution.py:26
  7.8 3.1 %collective-permute-start.4 = (f32[2,144,128]{2,1,0:T(8,128)S(1)}, f32[2,144,128]{2,1,0:T(8,128)S(1)}, u32[]{:S(2)}, u32[]{:S(2)}) collective-permute-start(f32[2,144,128]{2,1,0:T(8,128)S(1)} %pad_maximum_fusion.4), channel_id=1, source_target_pairs={{0,8},{4,12},{8,16},{12,20},{16,24},{20,28},{24,0},{28,4},{1,9},{5... | collective-permute-start | bytes 442376 | tf_op jit(solution)/shard_map/ppermute | solution.py:26
  10.9 3.1 %collective-permute-start.5 = (f32[2,144,128]{2,1,0:T(8,128)S(1)}, f32[2,144,128]{2,1,0:T(8,128)S(1)}, u32[]{:S(2)}, u32[]{:S(2)}) collective-permute-start(f32[2,144,128]{2,1,0:T(8,128)S(1)} %pad_maximum_fusion.4), channel_id=1, source_target_pairs={{0,24},{4,28},{8,0},{12,4},{16,8},{20,12},{24,16},{28,20},{1,25},{... | collective-permute-start | bytes 442376 | tf_op jit(solution)/shard_map/ppermute | solution.py:26
  14.0 2.1 %collective-permute-start.12 = (f32[88,1024]{1,0:T(8,128)}, f32[88,1024]{1,0:T(8,128)S(1)}, u32[]{:S(2)}, u32[]{:S(2)}) collective-permute-start(f32[88,1024]{1,0:T(8,128)} %get-tuple-element.27), channel_id=1, source_target_pairs={{0,32},{32,0},{1,33},{33,1},{2,34},{34,2},{3,35},{35,3},{4,36},{36... | collective-permute-start | bytes 1081352 | tf_op jit(solution)/shard_map/ppermute | solution.py:26
  19.4 4.9 %collective-permute-start.6 = (f32[2,144,128]{2,1,0:T(8,128)S(1)}, f32[2,144,128]{2,1,0:T(8,128)S(1)}, u32[]{:S(2)}, u32[]{:S(2)}) collective-permute-start(f32[2,144,128]{2,1,0:T(8,128)S(1)} %pad_maximum_fusion.4), channel_id=1, source_target_pairs={{0,16},{4,20},{8,24},{12,28},{16,0},{20,4},{24,8},{28,12},{1,17},{... | collective-permute-start | bytes 442376 | tf_op jit(solution)/shard_map/ppermute | solution.py:26
  25.5 4.8 %collective-permute-done.6 = f32[2,144,128]{2,1,0:T(8,128)S(1)} collective-permute-done((f32[2,144,128]{2,1,0:T(8,128)S(1)}, f32[2,144,128]{2,1,0:T(8,128)S(1)}, u32[]{:S(2)}, u32[]{:S(2)}) %collective-permute-start.6) | collective-permute-done | bytes 147488 | tf_op jit(solution)/shard_map/ppermute | solution.py:26
  30.3 2.7 %collective-permute-start.2 = (f32[128,1024]{1,0:T(8,128)}, f32[128,1024]{1,0:T(8,128)S(1)}, u32[]{:S(2)}, u32[]{:S(2)}) collective-permute-start(f32[128,1024]{1,0:T(8,128)} %tgt_ref.1), channel_id=1, source_target_pairs={{0,128},{64,192},{128,0},{192,64},{1,129},{65,193},{129,1},{193,65... | collective-permute-start | bytes 1572872 | tf_op jit(solution)/shard_map/ppermute | solution.py:26
  33.1 4.7 %collective-permute-start.8 = (f32[4,144,128]{2,1,0:T(8,128)S(1)}, f32[4,144,128]{2,1,0:T(8,128)S(1)}, u32[]{:S(2)}, u32[]{:S(2)}) collective-permute-start(f32[4,144,128]{2,1,0:T(8,128)S(1)} %get-tuple-element.43), channel_id=1, source_target_pairs={{0,28},{4,0},{8,4},{12,8},{16,12},{20,16},{24,20},{28,24},{1,29},{... | collective-permute-start | bytes 884744 | tf_op jit(solution)/shard_map/ppermute | solution.py:26
  38.8 2.5 %collective-permute-start.15 = (f32[88,1024]{1,0:T(8,128)S(1)}, f32[88,1024]{1,0:T(8,128)S(1)}, u32[]{:S(2)}, u32[]{:S(2)}) collective-permute-start(f32[88,1024]{1,0:T(8,128)S(1)} %select_maximum_fusion.refs_1_), channel_id=1, source_target_pairs={{0,192},{64,0},{128,64},{192,128},{1,193},{65,1},{129,65},{193,129... | collective-permute-start | bytes 1081352 | tf_op jit(solution)/shard_map/ppermute | solution.py:26
  42.1 2.2 %collective-permute-start.13 = (f32[96,1024]{1,0:T(8,128)S(1)}, f32[96,1024]{1,0:T(8,128)S(1)}, u32[]{:S(2)}, u32[]{:S(2)}) collective-permute-start(f32[96,1024]{1,0:T(8,128)S(1)} %pad_maximum_fusion.1), channel_id=1, source_target_pairs={{0,32},{32,0},{1,33},{33,1},{2,34},{34,2},{3,35},{35,3},{4,36},{36... | collective-permute-start | bytes 1179656 | tf_op jit(solution)/shard_map/ppermute | solution.py:26
  45.7 7.6 %collective-permute-done.14.refs_3_ = f32[88,1024]{1,0:T(8,128)S(1)} collective-permute-done((f32[88,1024]{1,0:T(8,128)S(1)}, f32[88,1024]{1,0:T(8,128)S(1)}, u32[]{:S(2)}, u32[]{:S(2)}) %collective-permute-start.14) | collective-permute-done | bytes 360480 | tf_op jit(solution)/shard_map/ppermute | solution.py:26
  54.4 2.4 %collective-permute-start.11 = (f32[48,1024]{1,0:T(8,128)S(1)}, f32[48,1024]{1,0:T(8,128)S(1)}, u32[]{:S(2)}, u32[]{:S(2)}) collective-permute-start(f32[48,1024]{1,0:T(8,128)S(1)} %copy-done.2), channel_id=1, source_target_pairs={{0,32},{32,0},{1,33},{33,1},{2,34},{34,2},{3,35},{35,3},{4,36},{36... | collective-permute-start | bytes 589832 | tf_op jit(solution)/shard_map/ppermute | solution.py:26
  58.5 3.5 %collective-permute-start.16 = (f32[48,1024]{1,0:T(8,128)S(1)}, f32[48,1024]{1,0:T(8,128)S(1)}, u32[]{:S(2)}, u32[]{:S(2)}) collective-permute-start(f32[48,1024]{1,0:T(8,128)S(1)} %slice.174), channel_id=1, source_target_pairs={{0,32},{32,0},{1,33},{33,1},{2,34},{34,2},{3,35},{35,3},{4,36},{36... | collective-permute-start | bytes 589832 | tf_op jit(solution)/shard_map/ppermute | solution.py:26
  62.6 2.0 %shard_map.49 = (f32[512,512]{1,0:T(8,128)S(1)}, f32[8,128]{1,0:T(8,128)S(1)}) custom-call(bf16[512,1024]{1,0:T(8,128)(2,1)S(1)} %get-tuple-element.19.refs_0_, bf16[512,1024]{1,0:T(8,128)(2,1)S(1)} %get-tuple-element.20.refs_1_, bf16[512,1024]{1,0:T(8,128)(2,1)S(1)} %get-tuple-element.22.refs_2_.refs_8_, ...), custom_call_target="tpu_custom_call" | custom-call | flops 1610612736 | bytes 6291456 | tf_op jit(solution)/shard_map/pallas_call | solution.py:226
  64.7 2.3 %collective-permute-done.16.refs_6_ = f32[48,1024]{1,0:T(8,128)S(1)} collective-permute-done((f32[48,1024]{1,0:T(8,128)S(1)}, f32[48,1024]{1,0:T(8,128)S(1)}, u32[]{:S(2)}, u32[]{:S(2)}) %collective-permute-start.16) | collective-permute-done | bytes 196640 | tf_op jit(solution)/shard_map/ppermute | solution.py:26
  67.0 3.1 %shard_map.50 = (f32[512,512]{1,0:T(8,128)S(1)}, f32[8,128]{1,0:T(8,128)S(1)}, f32[16,128]{1,0:T(8,128)S(1)}, f32[8,128]{1,0:T(8,128)S(1)}) custom-call(f32[48,1024]{1,0:T(8,128)S(1)} %collective-permute-done.11.refs_0_, f32[88,1024]{1,0:T(8,128)S(1)} %select_maximum_fusion.refs_1_, f32[48,1024]{1,0:T(8,128)S(1)} %get-tuple-element.42.refs_2_, ...), custom_call_target="tpu_custom_call" | custom-call | flops 1610612736 | bytes 6291456 | tf_op jit(solution)/shard_map/pallas_call | solution.py:226
  71.4 6.4 %collective-permute-start.19 = (f32[8,128]{1,0:T(8,128)S(1)}, f32[8,128]{1,0:T(8,128)S(1)}, u32[]{:S(2)}, u32[]{:S(2)}) collective-permute-start(f32[8,128]{1,0:T(8,128)S(1)} %pad_maximum_fusion.7), channel_id=1, source_target_pairs={{0,8},{4,12},{8,16},{12,20},{16,24},{20,28},{24,0},{28,4},{1,9},{5... | collective-permute-start | bytes 12296 | tf_op jit(solution)/shard_map/ppermute | solution.py:26
  77.8 3.7 %collective-permute-start.21 = (f32[8,128]{1,0:T(8,128)S(1)}, f32[8,128]{1,0:T(8,128)S(1)}, u32[]{:S(2)}, u32[]{:S(2)}) collective-permute-start(f32[8,128]{1,0:T(8,128)S(1)} %pad_maximum_fusion.7), channel_id=1, source_target_pairs={{0,16},{4,20},{8,24},{12,28},{16,0},{20,4},{24,8},{28,12},{1,17},{... | collective-permute-start | bytes 12296 | tf_op jit(solution)/shard_map/ppermute | solution.py:26
  82.2 2.5 %collective-permute-start.26 = (f32[16,128]{1,0:T(8,128)S(1)}, f32[16,128]{1,0:T(8,128)S(1)}, u32[]{:S(2)}, u32[]{:S(2)}) collective-permute-start(f32[16,128]{1,0:T(8,128)S(1)} %get-tuple-element.32), channel_id=1, source_target_pairs={{0,192},{64,0},{128,64},{192,128},{1,193},{65,1},{129,65},{193,129... | collective-permute-start | bytes 24584 | tf_op jit(solution)/shard_map/ppermute | solution.py:26
  87.2 2.2 %collective-permute-start.24 = (f32[8,128]{1,0:T(8,128)S(1)}, f32[8,128]{1,0:T(8,128)S(1)}, u32[]{:S(2)}, u32[]{:S(2)}) collective-permute-start(f32[8,128]{1,0:T(8,128)S(1)} %pad_maximum_fusion.8), channel_id=1, source_target_pairs={{0,6},{2,4},{4,2},{6,0},{8,14},{10,12},{12,10},{14,8},{16,22},{18,... | collective-permute-start | bytes 12296 | tf_op jit(solution)/shard_map/ppermute | solution.py:318
  91.8 3.4 %collective-permute-done.28 = f32[16,128]{1,0:T(8,128)S(1)} collective-permute-done((f32[16,128]{1,0:T(8,128)S(1)}, f32[16,128]{1,0:T(8,128)S(1)}, u32[]{:S(2)}, u32[]{:S(2)}) %collective-permute-start.28) | collective-permute-done | bytes 8224 | tf_op jit(solution)/shard_map/ppermute | solution.py:26
  95.2 2.6 %shard_map.51 = f32[512,1024]{1,0:T(8,128)} custom-call(f32[512,512]{1,0:T(8,128)S(1)} %get-tuple-element.25.refs_12_.same_ref, f32[512,512]{1,0:T(8,128)S(1)} %get-tuple-element.29.other_ref, f32[512,128]{1,0:T(8,128)S(1)} %get-tuple-element.24.refs_4_.refs_10_.inv_ref, f32[8,128]{1,0:T(8,128)S(1)} %get-tuple-element.30.tinv_ref, ...), custom_call_target="tpu_custom_call" | custom-call | tf_op jit(solution)/shard_map/pallas_call | solution.py:264
  (72 shorter events, 18.6 us)
Async XLA Ops:
  7.8 11.6 %collective-permute-start.4 = (f32[2,144,128]{2,1,0:T(8,128)S(1)}, f32[2,144,128]{2,1,0:T(8,128)S(1)}, u32[]{:S(2)}, u32[]{:S(2)}) collective-permute-start(f32[2,144,128]{2,1,0:T(8,128)S(1)} %pad_maximum_fusion.4), channel_id=1, source_target_pairs={{0,8},{4,12},{8,16},{12,20},{16,24},{20,28},{24,0},{28,4},{1,9},{5... | collective-permute-start | bytes 442376 | tf_op jit(solution)/shard_map/ppermute | solution.py:26
  10.9 13.4 %collective-permute-start.5 = (f32[2,144,128]{2,1,0:T(8,128)S(1)}, f32[2,144,128]{2,1,0:T(8,128)S(1)}, u32[]{:S(2)}, u32[]{:S(2)}) collective-permute-start(f32[2,144,128]{2,1,0:T(8,128)S(1)} %pad_maximum_fusion.4), channel_id=1, source_target_pairs={{0,24},{4,28},{8,0},{12,4},{16,8},{20,12},{24,16},{28,20},{1,25},{... | collective-permute-start | bytes 442376 | tf_op jit(solution)/shard_map/ppermute | solution.py:26
  14.0 19.1 %collective-permute-start.12 = (f32[88,1024]{1,0:T(8,128)}, f32[88,1024]{1,0:T(8,128)S(1)}, u32[]{:S(2)}, u32[]{:S(2)}) collective-permute-start(f32[88,1024]{1,0:T(8,128)} %get-tuple-element.27), channel_id=1, source_target_pairs={{0,32},{32,0},{1,33},{33,1},{2,34},{34,2},{3,35},{35,3},{4,36},{36... | collective-permute-start | bytes 1081352 | tf_op jit(solution)/shard_map/ppermute | solution.py:26
  16.2 22.6 %collective-permute-start = (f32[128,1024]{1,0:T(8,128)}, f32[128,1024]{1,0:T(8,128)S(1)}, u32[]{:S(2)}, u32[]{:S(2)}) collective-permute-start(f32[128,1024]{1,0:T(8,128)} %tgt_ref.1), channel_id=1, source_target_pairs={{0,64},{64,128},{128,192},{192,0},{1,65},{65,129},{129,193},{193,1... | collective-permute-start | bytes 1572872 | tf_op jit(solution)/shard_map/ppermute | solution.py:26
  17.7 23.6 %collective-permute-start.1 = (f32[128,1024]{1,0:T(8,128)}, f32[128,1024]{1,0:T(8,128)S(1)}, u32[]{:S(2)}, u32[]{:S(2)}) collective-permute-start(f32[128,1024]{1,0:T(8,128)} %tgt_ref.1), channel_id=1, source_target_pairs={{0,192},{64,0},{128,64},{192,128},{1,193},{65,1},{129,65},{193,129... | collective-permute-start | bytes 1572872 | tf_op jit(solution)/shard_map/ppermute | solution.py:26
  19.4 10.9 %collective-permute-start.6 = (f32[2,144,128]{2,1,0:T(8,128)S(1)}, f32[2,144,128]{2,1,0:T(8,128)S(1)}, u32[]{:S(2)}, u32[]{:S(2)}) collective-permute-start(f32[2,144,128]{2,1,0:T(8,128)S(1)} %pad_maximum_fusion.4), channel_id=1, source_target_pairs={{0,16},{4,20},{8,24},{12,28},{16,0},{20,4},{24,8},{28,12},{1,17},{... | collective-permute-start | bytes 442376 | tf_op jit(solution)/shard_map/ppermute | solution.py:26
  24.4 13.5 %collective-permute-start.7 = (f32[4,144,128]{2,1,0:T(8,128)S(1)}, f32[4,144,128]{2,1,0:T(8,128)S(1)}, u32[]{:S(2)}, u32[]{:S(2)}) collective-permute-start(f32[4,144,128]{2,1,0:T(8,128)S(1)} %get-tuple-element.44), channel_id=1, source_target_pairs={{0,4},{4,8},{8,12},{12,16},{16,20},{20,24},{24,28},{28,0},{1,5},{5... | collective-permute-start | bytes 884744 | tf_op jit(solution)/shard_map/ppermute | solution.py:26
  30.3 15.4 %collective-permute-start.2 = (f32[128,1024]{1,0:T(8,128)}, f32[128,1024]{1,0:T(8,128)S(1)}, u32[]{:S(2)}, u32[]{:S(2)}) collective-permute-start(f32[128,1024]{1,0:T(8,128)} %tgt_ref.1), channel_id=1, source_target_pairs={{0,128},{64,192},{128,0},{192,64},{1,129},{65,193},{129,1},{193,65... | collective-permute-start | bytes 1572872 | tf_op jit(solution)/shard_map/ppermute | solution.py:26
  33.1 9.0 %collective-permute-start.8 = (f32[4,144,128]{2,1,0:T(8,128)S(1)}, f32[4,144,128]{2,1,0:T(8,128)S(1)}, u32[]{:S(2)}, u32[]{:S(2)}) collective-permute-start(f32[4,144,128]{2,1,0:T(8,128)S(1)} %get-tuple-element.43), channel_id=1, source_target_pairs={{0,28},{4,0},{8,4},{12,8},{16,12},{20,16},{24,20},{28,24},{1,29},{... | collective-permute-start | bytes 884744 | tf_op jit(solution)/shard_map/ppermute | solution.py:26
  37.9 15.4 %collective-permute-start.14 = (f32[88,1024]{1,0:T(8,128)S(1)}, f32[88,1024]{1,0:T(8,128)S(1)}, u32[]{:S(2)}, u32[]{:S(2)}) collective-permute-start(f32[88,1024]{1,0:T(8,128)S(1)} %select_maximum_fusion.refs_1_), channel_id=1, source_target_pairs={{0,64},{64,128},{128,192},{192,0},{1,65},{65,129},{129,193},{193,1... | collective-permute-start | bytes 1081352 | tf_op jit(solution)/shard_map/ppermute | solution.py:26
  38.8 15.6 %collective-permute-start.15 = (f32[88,1024]{1,0:T(8,128)S(1)}, f32[88,1024]{1,0:T(8,128)S(1)}, u32[]{:S(2)}, u32[]{:S(2)}) collective-permute-start(f32[88,1024]{1,0:T(8,128)S(1)} %select_maximum_fusion.refs_1_), channel_id=1, source_target_pairs={{0,192},{64,0},{128,64},{192,128},{1,193},{65,1},{129,65},{193,129... | collective-permute-start | bytes 1081352 | tf_op jit(solution)/shard_map/ppermute | solution.py:26
  41.3 17.1 %collective-permute-start.17 = (f32[88,1024]{1,0:T(8,128)S(1)}, f32[88,1024]{1,0:T(8,128)S(1)}, u32[]{:S(2)}, u32[]{:S(2)}) collective-permute-start(f32[88,1024]{1,0:T(8,128)S(1)} %select_maximum_fusion.refs_1_), channel_id=1, source_target_pairs={{0,128},{64,192},{128,0},{192,64},{1,129},{65,193},{129,1},{193,65... | collective-permute-start | bytes 1081352 | tf_op jit(solution)/shard_map/ppermute | solution.py:26
  42.1 19.9 %collective-permute-start.13 = (f32[96,1024]{1,0:T(8,128)S(1)}, f32[96,1024]{1,0:T(8,128)S(1)}, u32[]{:S(2)}, u32[]{:S(2)}) collective-permute-start(f32[96,1024]{1,0:T(8,128)S(1)} %pad_maximum_fusion.1), channel_id=1, source_target_pairs={{0,32},{32,0},{1,33},{33,1},{2,34},{34,2},{3,35},{35,3},{4,36},{36... | collective-permute-start | bytes 1179656 | tf_op jit(solution)/shard_map/ppermute | solution.py:26
  45.7 16.3 %collective-permute-start.9 = (f32[8,144,128]{2,1,0:T(8,128)S(1)}, f32[8,144,128]{2,1,0:T(8,128)S(1)}, u32[]{:S(2)}, u32[]{:S(2)}) collective-permute-start(f32[8,144,128]{2,1,0:T(8,128)S(1)} %pad_maximum_fusion.refs_0_), channel_id=1, source_target_pairs={{0,1},{1,0},{2,3},{3,2},{4,5},{5,4},{6,7},{7,6},{8,9},{9,8},{10,11... | collective-permute-start | bytes 1769480 | tf_op jit(solution)/shard_map/ppermute | solution.py:26
  53.3 8.7 %collective-permute-start.10 = (f32[8,144,128]{2,1,0:T(8,128)S(1)}, f32[8,144,128]{2,1,0:T(8,128)S(1)}, u32[]{:S(2)}, u32[]{:S(2)}) collective-permute-start(f32[8,144,128]{2,1,0:T(8,128)S(1)} %constant_dynamic-update-slice_fusion.refs_1_), channel_id=1, source_target_pairs={{0,1},{1,0},{2,3},{3,2},{4,5},{5,4},{6,7},{7,6},{8,9},{9,8},{10,11... | collective-permute-start | bytes 1769480 | tf_op jit(solution)/shard_map/ppermute | solution.py:26
  54.4 10.2 %collective-permute-start.11 = (f32[48,1024]{1,0:T(8,128)S(1)}, f32[48,1024]{1,0:T(8,128)S(1)}, u32[]{:S(2)}, u32[]{:S(2)}) collective-permute-start(f32[48,1024]{1,0:T(8,128)S(1)} %copy-done.2), channel_id=1, source_target_pairs={{0,32},{32,0},{1,33},{33,1},{2,34},{34,2},{3,35},{35,3},{4,36},{36... | collective-permute-start | bytes 589832 | tf_op jit(solution)/shard_map/ppermute | solution.py:26
  58.5 8.5 %collective-permute-start.16 = (f32[48,1024]{1,0:T(8,128)S(1)}, f32[48,1024]{1,0:T(8,128)S(1)}, u32[]{:S(2)}, u32[]{:S(2)}) collective-permute-start(f32[48,1024]{1,0:T(8,128)S(1)} %slice.174), channel_id=1, source_target_pairs={{0,32},{32,0},{1,33},{33,1},{2,34},{34,2},{3,35},{35,3},{4,36},{36... | collective-permute-start | bytes 589832 | tf_op jit(solution)/shard_map/ppermute | solution.py:26
  71.4 13.3 %collective-permute-start.19 = (f32[8,128]{1,0:T(8,128)S(1)}, f32[8,128]{1,0:T(8,128)S(1)}, u32[]{:S(2)}, u32[]{:S(2)}) collective-permute-start(f32[8,128]{1,0:T(8,128)S(1)} %pad_maximum_fusion.7), channel_id=1, source_target_pairs={{0,8},{4,12},{8,16},{12,20},{16,24},{20,28},{24,0},{28,4},{1,9},{5... | collective-permute-start | bytes 12296 | tf_op jit(solution)/shard_map/ppermute | solution.py:26
  77.8 8.0 %collective-permute-start.20 = (f32[8,128]{1,0:T(8,128)S(1)}, f32[8,128]{1,0:T(8,128)S(1)}, u32[]{:S(2)}, u32[]{:S(2)}) collective-permute-start(f32[8,128]{1,0:T(8,128)S(1)} %pad_maximum_fusion.7), channel_id=1, source_target_pairs={{0,24},{4,28},{8,0},{12,4},{16,8},{20,12},{24,16},{28,20},{1,25},{... | collective-permute-start | bytes 12296 | tf_op jit(solution)/shard_map/ppermute | solution.py:26
  77.8 8.0 %collective-permute-start.21 = (f32[8,128]{1,0:T(8,128)S(1)}, f32[8,128]{1,0:T(8,128)S(1)}, u32[]{:S(2)}, u32[]{:S(2)}) collective-permute-start(f32[8,128]{1,0:T(8,128)S(1)} %pad_maximum_fusion.7), channel_id=1, source_target_pairs={{0,16},{4,20},{8,24},{12,28},{16,0},{20,4},{24,8},{28,12},{1,17},{... | collective-permute-start | bytes 12296 | tf_op jit(solution)/shard_map/ppermute | solution.py:26
  81.5 5.8 %collective-permute-start.25 = (f32[16,128]{1,0:T(8,128)S(1)}, f32[16,128]{1,0:T(8,128)S(1)}, u32[]{:S(2)}, u32[]{:S(2)}) collective-permute-start(f32[16,128]{1,0:T(8,128)S(1)} %get-tuple-element.32), channel_id=1, source_target_pairs={{0,64},{64,128},{128,192},{192,0},{1,65},{65,129},{129,193},{193,1... | collective-permute-start | bytes 24584 | tf_op jit(solution)/shard_map/ppermute | solution.py:26
  82.2 7.2 %collective-permute-start.26 = (f32[16,128]{1,0:T(8,128)S(1)}, f32[16,128]{1,0:T(8,128)S(1)}, u32[]{:S(2)}, u32[]{:S(2)}) collective-permute-start(f32[16,128]{1,0:T(8,128)S(1)} %get-tuple-element.32), channel_id=1, source_target_pairs={{0,192},{64,0},{128,64},{192,128},{1,193},{65,1},{129,65},{193,129... | collective-permute-start | bytes 24584 | tf_op jit(solution)/shard_map/ppermute | solution.py:26
  85.8 5.9 %collective-permute-start.22 = (f32[8,128]{1,0:T(8,128)S(1)}, f32[8,128]{1,0:T(8,128)S(1)}, u32[]{:S(2)}, u32[]{:S(2)}) collective-permute-start(f32[8,128]{1,0:T(8,128)S(1)} %pad_maximum_fusion.8), channel_id=1, source_target_pairs={{0,4},{4,0},{8,12},{12,8},{16,20},{20,16},{24,28},{28,24},{1,5},{5... | collective-permute-start | bytes 12296 | tf_op jit(solution)/shard_map/ppermute | solution.py:317
  86.4 5.3 %collective-permute-start.23 = (f32[8,128]{1,0:T(8,128)S(1)}, f32[8,128]{1,0:T(8,128)S(1)}, u32[]{:S(2)}, u32[]{:S(2)}) collective-permute-start(f32[8,128]{1,0:T(8,128)S(1)} %pad_maximum_fusion.8), channel_id=1, source_target_pairs={{0,2},{2,0},{1,3},{3,1},{4,6},{6,4},{5,7},{7,5},{8,10},{10,8},{9,1... | collective-permute-start | bytes 12296 | tf_op jit(solution)/shard_map/ppermute | solution.py:26
  (8 other events, 92.2 us)

commit v4 on v3

--- a/solution.py
+++ b/solution.py
@@ -190,7 +190,7 @@
     sims += dot(hi_ref[...], blo[...], NT)
     sims += dot(lo_ref[...], bhi[...], NT)
     sims_ref[...] = sims
-    inv = inv_ref[:, :1]
+    inv = jnp.concatenate([inv_ref[...]] * 4, axis=1)
     logits = sims * inv
     top = jnp.max(logits, axis=1, keepdims=True)
     total = jnp.sum(jnp.exp(logits - top), axis=1, keepdims=True)
@@ -236,20 +236,21 @@
     )(*operands)
 
 
-def final_kernel(same_ref, other_ref, inv_ref, tinv_ref, row_ref, col_ref, out_ref, held, sems):
+def final_kernel(same_ref, other_ref, inv_ref, tinv_ref, row_ref, col_ref, out_ref, held, rows, sems):
     xh = lax.axis_index("xh")
     row = from_lanes(row_ref[0:4, :] + jnp.log(row_ref[4:8, :])) - math.log(32768)
-    inv = inv_ref[:, :1]
+    rows[...] = jnp.broadcast_to(row, (512, LANES))
     col = col_ref[0:8, :] + jnp.log(col_ref[8:16, :]) - math.log(4096)
     copies = []
     for side, sims_ref in enumerate((same_ref, other_ref)):
         for j in range(4):
             k = 4 * side + j
             right = col[4 * side + j : 4 * side + j + 1, :]
-            top = jnp.maximum(row, right)
-            gap = jnp.minimum(row, right) - top
+            left = rows[...]
+            top = jnp.maximum(left, right)
+            gap = jnp.minimum(left, right) - top
             both = top + jnp.log(1.0 + jnp.exp(gap)) - math.log(2.0)
-            scale = 0.5 * (inv + tinv_ref[4 * side + j : 4 * side + j + 1, :])
+            scale = 0.5 * (inv_ref[...] + tinv_ref[4 * side + j : 4 * side + j + 1, :])
             sims = sims_ref[:, j * LANES : (j + 1) * LANES]
             held[k] = sims * scale - both
             place = pl.multiple_of((2 * j + (xh ^ side)) * LANES, LANES)
@@ -266,7 +267,7 @@
         out_shape=jax.ShapeDtypeStruct((512, 1024), jnp.float32),
         in_specs=[whole()] * 6,
         out_specs=pl.BlockSpec(memory_space=pl.ANY),
-        scratch_shapes=[pltpu.VMEM((8, 512, LANES), jnp.float32), pltpu.SemaphoreType.DMA((8,))],
+        scratch_shapes=[pltpu.VMEM((8, 512, LANES), jnp.float32), pltpu.VMEM((512, LANES), jnp.float32), pltpu.SemaphoreType.DMA((8,))],
         compiler_params=pltpu.CompilerParams(vmem_limit_bytes=24 << 20),
     )(*operands)
 

time: 98 us -> 98 us (level)
  no operation moved by 1% of the time
where the time goes in v4:
time: 98 us; the launch traced here: 97.8 us
  starting transfers between devices  58.9 us (60%)
  waiting for transfers between devices  26.5 us (27%)
  Pallas kernels  10.7 us (11%)
  other arithmetic  1.15 us (1%)
    ppermute x27, starting transfers between devices, shifted(): return lax.ppermute(value, axis, [(i, (i + by) % n) for i in range(n)])  56.1 us
    ppermute x27, waiting for transfers between devices, shifted(): return lax.ppermute(value, axis, [(i, (i + by) % n) for i in range(n)])  26.5 us
    pallas_call x2, Pallas kernels, tile(): pl.pallas_call(functools.partial(tile_kernel, side), out_shape=shapes, in...  5.19 us
    pallas_call x1, Pallas kernels, final(): pl.pallas_call(final_kernel, out_shape=jax.ShapeDtypeStruct((512, 1024),...  2.53 us
    ppermute x1, starting transfers between devices, all_rows(): lax.ppermute(row, ('z', 'xl'), [(2 * i + k, 2 * (i ^ 1) + (k ^ 1)) for i...  2.17 us
    pallas_call x1, Pallas kernels, first_blocks(): pl.pallas_call(first_kernel, out_shape=(jax.ShapeDtypeStruct((144, LANES)...  2 us
  transfers between devices with their start and end apart: 29, of which 11 were waited for; matrix products, arithmetic and copies ran while one was open for 0% of the time, Pallas kernels for 3%

profile of v4, /device:TPU:2, one launch (start us, length us, event | category | flops | bytes accessed | tf_op | source)
XLA Modules:
  0.0 97.8 jit_solution(11728072616059729452)
XLA Ops:
  0.0 2.0 %shard_map.47 = (f32[144,128]{1,0:T(8,128)}, f32[88,1024]{1,0:T(8,128)}, f32[48,1024]{1,0:T(8,128)}) custom-call(f32[16,1024]{1,0:T(8,128)} %src_ref.1, f32[1,16]{1,0:T(1,128)} %bitcast.10, f32[128,1024]{1,0:T(8,128)} %tgt_ref.1, f32[1,128]{1,0:T(1,128)} %bitcast.8), custom_call_target="tpu_custom_call" | custom-call | flops 65536 | bytes 1048576 | tf_op jit(solution)/shard_map/pallas_call | solution.py:62
  2.0 2.3 %collective-permute-start.3 = (f32[144,128]{1,0:T(8,128)}, f32[144,128]{1,0:T(8,128)S(1)}, u32[]{:S(2)}, u32[]{:S(2)}) collective-permute-start(f32[144,128]{1,0:T(8,128)} %get-tuple-element.21), channel_id=1, source_target_pairs={{0,2},{2,0},{1,3},{3,1},{4,6},{6,4},{5,7},{7,5},{8,10},{10,8},{9,1... | collective-permute-start | bytes 221192 | tf_op jit(solution)/shard_map/ppermute | solution.py:26
  4.3 2.5 %collective-permute-done.3 = f32[144,128]{1,0:T(8,128)S(1)} collective-permute-done((f32[144,128]{1,0:T(8,128)}, f32[144,128]{1,0:T(8,128)S(1)}, u32[]{:S(2)}, u32[]{:S(2)}) %collective-permute-start.3) | collective-permute-done | bytes 73760 | tf_op jit(solution)/shard_map/ppermute | solution.py:26
  7.8 3.1 %collective-permute-start.4 = (f32[2,144,128]{2,1,0:T(8,128)S(1)}, f32[2,144,128]{2,1,0:T(8,128)S(1)}, u32[]{:S(2)}, u32[]{:S(2)}) collective-permute-start(f32[2,144,128]{2,1,0:T(8,128)S(1)} %pad_maximum_fusion.4), channel_id=1, source_target_pairs={{0,8},{4,12},{8,16},{12,20},{16,24},{20,28},{24,0},{28,4},{1,9},{5... | collective-permute-start | bytes 442376 | tf_op jit(solution)/shard_map/ppermute | solution.py:26
  10.9 3.1 %collective-permute-start.5 = (f32[2,144,128]{2,1,0:T(8,128)S(1)}, f32[2,144,128]{2,1,0:T(8,128)S(1)}, u32[]{:S(2)}, u32[]{:S(2)}) collective-permute-start(f32[2,144,128]{2,1,0:T(8,128)S(1)} %pad_maximum_fusion.4), channel_id=1, source_target_pairs={{0,24},{4,28},{8,0},{12,4},{16,8},{20,12},{24,16},{28,20},{1,25},{... | collective-permute-start | bytes 442376 | tf_op jit(solution)/shard_map/ppermute | solution.py:26
  14.0 2.1 %collective-permute-start.12 = (f32[88,1024]{1,0:T(8,128)}, f32[88,1024]{1,0:T(8,128)S(1)}, u32[]{:S(2)}, u32[]{:S(2)}) collective-permute-start(f32[88,1024]{1,0:T(8,128)} %get-tuple-element.27), channel_id=1, source_target_pairs={{0,32},{32,0},{1,33},{33,1},{2,34},{34,2},{3,35},{35,3},{4,36},{36... | collective-permute-start | bytes 1081352 | tf_op jit(solution)/shard_map/ppermute | solution.py:26
  19.4 4.9 %collective-permute-start.6 = (f32[2,144,128]{2,1,0:T(8,128)S(1)}, f32[2,144,128]{2,1,0:T(8,128)S(1)}, u32[]{:S(2)}, u32[]{:S(2)}) collective-permute-start(f32[2,144,128]{2,1,0:T(8,128)S(1)} %pad_maximum_fusion.4), channel_id=1, source_target_pairs={{0,16},{4,20},{8,24},{12,28},{16,0},{20,4},{24,8},{28,12},{1,17},{... | collective-permute-start | bytes 442376 | tf_op jit(solution)/shard_map/ppermute | solution.py:26
  25.5 4.8 %collective-permute-done.6 = f32[2,144,128]{2,1,0:T(8,128)S(1)} collective-permute-done((f32[2,144,128]{2,1,0:T(8,128)S(1)}, f32[2,144,128]{2,1,0:T(8,128)S(1)}, u32[]{:S(2)}, u32[]{:S(2)}) %collective-permute-start.6) | collective-permute-done | bytes 147488 | tf_op jit(solution)/shard_map/ppermute | solution.py:26
  30.3 2.7 %collective-permute-start.2 = (f32[128,1024]{1,0:T(8,128)}, f32[128,1024]{1,0:T(8,128)S(1)}, u32[]{:S(2)}, u32[]{:S(2)}) collective-permute-start(f32[128,1024]{1,0:T(8,128)} %tgt_ref.1), channel_id=1, source_target_pairs={{0,128},{64,192},{128,0},{192,64},{1,129},{65,193},{129,1},{193,65... | collective-permute-start | bytes 1572872 | tf_op jit(solution)/shard_map/ppermute | solution.py:26
  33.1 4.7 %collective-permute-start.8 = (f32[4,144,128]{2,1,0:T(8,128)S(1)}, f32[4,144,128]{2,1,0:T(8,128)S(1)}, u32[]{:S(2)}, u32[]{:S(2)}) collective-permute-start(f32[4,144,128]{2,1,0:T(8,128)S(1)} %get-tuple-element.43), channel_id=1, source_target_pairs={{0,28},{4,0},{8,4},{12,8},{16,12},{20,16},{24,20},{28,24},{1,29},{... | collective-permute-start | bytes 884744 | tf_op jit(solution)/shard_map/ppermute | solution.py:26
  38.8 2.5 %collective-permute-start.15 = (f32[88,1024]{1,0:T(8,128)S(1)}, f32[88,1024]{1,0:T(8,128)S(1)}, u32[]{:S(2)}, u32[]{:S(2)}) collective-permute-start(f32[88,1024]{1,0:T(8,128)S(1)} %select_maximum_fusion.refs_1_), channel_id=1, source_target_pairs={{0,192},{64,0},{128,64},{192,128},{1,193},{65,1},{129,65},{193,129... | collective-permute-start | bytes 1081352 | tf_op jit(solution)/shard_map/ppermute | solution.py:26
  42.1 2.2 %collective-permute-start.13 = (f32[96,1024]{1,0:T(8,128)S(1)}, f32[96,1024]{1,0:T(8,128)S(1)}, u32[]{:S(2)}, u32[]{:S(2)}) collective-permute-start(f32[96,1024]{1,0:T(8,128)S(1)} %pad_maximum_fusion.1), channel_id=1, source_target_pairs={{0,32},{32,0},{1,33},{33,1},{2,34},{34,2},{3,35},{35,3},{4,36},{36... | collective-permute-start | bytes 1179656 | tf_op jit(solution)/shard_map/ppermute | solution.py:26
  45.7 7.6 %collective-permute-done.14.refs_3_ = f32[88,1024]{1,0:T(8,128)S(1)} collective-permute-done((f32[88,1024]{1,0:T(8,128)S(1)}, f32[88,1024]{1,0:T(8,128)S(1)}, u32[]{:S(2)}, u32[]{:S(2)}) %collective-permute-start.14) | collective-permute-done | bytes 360480 | tf_op jit(solution)/shard_map/ppermute | solution.py:26
  54.4 2.4 %collective-permute-start.11 = (f32[48,1024]{1,0:T(8,128)S(1)}, f32[48,1024]{1,0:T(8,128)S(1)}, u32[]{:S(2)}, u32[]{:S(2)}) collective-permute-start(f32[48,1024]{1,0:T(8,128)S(1)} %copy-done.2), channel_id=1, source_target_pairs={{0,32},{32,0},{1,33},{33,1},{2,34},{34,2},{3,35},{35,3},{4,36},{36... | collective-permute-start | bytes 589832 | tf_op jit(solution)/shard_map/ppermute | solution.py:26
  58.5 3.5 %collective-permute-start.16 = (f32[48,1024]{1,0:T(8,128)S(1)}, f32[48,1024]{1,0:T(8,128)S(1)}, u32[]{:S(2)}, u32[]{:S(2)}) collective-permute-start(f32[48,1024]{1,0:T(8,128)S(1)} %slice.174), channel_id=1, source_target_pairs={{0,32},{32,0},{1,33},{33,1},{2,34},{34,2},{3,35},{35,3},{4,36},{36... | collective-permute-start | bytes 589832 | tf_op jit(solution)/shard_map/ppermute | solution.py:26
  62.6 2.0 %shard_map.49 = (f32[512,512]{1,0:T(8,128)S(1)}, f32[8,128]{1,0:T(8,128)S(1)}) custom-call(bf16[512,1024]{1,0:T(8,128)(2,1)S(1)} %get-tuple-element.19.refs_0_, bf16[512,1024]{1,0:T(8,128)(2,1)S(1)} %get-tuple-element.20.refs_1_, bf16[512,1024]{1,0:T(8,128)(2,1)S(1)} %get-tuple-element.22.refs_2_.refs_8_, ...), custom_call_target="tpu_custom_call" | custom-call | flops 1610612736 | bytes 6291456 | tf_op jit(solution)/shard_map/pallas_call | solution.py:226
  64.7 2.3 %collective-permute-done.16.refs_6_ = f32[48,1024]{1,0:T(8,128)S(1)} collective-permute-done((f32[48,1024]{1,0:T(8,128)S(1)}, f32[48,1024]{1,0:T(8,128)S(1)}, u32[]{:S(2)}, u32[]{:S(2)}) %collective-permute-start.16) | collective-permute-done | bytes 196640 | tf_op jit(solution)/shard_map/ppermute | solution.py:26
  67.0 3.1 %shard_map.50 = (f32[512,512]{1,0:T(8,128)S(1)}, f32[8,128]{1,0:T(8,128)S(1)}, f32[16,128]{1,0:T(8,128)S(1)}, f32[8,128]{1,0:T(8,128)S(1)}) custom-call(f32[48,1024]{1,0:T(8,128)S(1)} %collective-permute-done.11.refs_0_, f32[88,1024]{1,0:T(8,128)S(1)} %select_maximum_fusion.refs_1_, f32[48,1024]{1,0:T(8,128)S(1)} %get-tuple-element.42.refs_2_, ...), custom_call_target="tpu_custom_call" | custom-call | flops 1610612736 | bytes 6291456 | tf_op jit(solution)/shard_map/pallas_call | solution.py:226
  71.4 6.4 %collective-permute-start.19 = (f32[8,128]{1,0:T(8,128)S(1)}, f32[8,128]{1,0:T(8,128)S(1)}, u32[]{:S(2)}, u32[]{:S(2)}) collective-permute-start(f32[8,128]{1,0:T(8,128)S(1)} %pad_maximum_fusion.7), channel_id=1, source_target_pairs={{0,8},{4,12},{8,16},{12,20},{16,24},{20,28},{24,0},{28,4},{1,9},{5... | collective-permute-start | bytes 12296 | tf_op jit(solution)/shard_map/ppermute | solution.py:26
  77.8 3.7 %collective-permute-start.21 = (f32[8,128]{1,0:T(8,128)S(1)}, f32[8,128]{1,0:T(8,128)S(1)}, u32[]{:S(2)}, u32[]{:S(2)}) collective-permute-start(f32[8,128]{1,0:T(8,128)S(1)} %pad_maximum_fusion.7), channel_id=1, source_target_pairs={{0,16},{4,20},{8,24},{12,28},{16,0},{20,4},{24,8},{28,12},{1,17},{... | collective-permute-start | bytes 12296 | tf_op jit(solution)/shard_map/ppermute | solution.py:26
  82.2 2.5 %collective-permute-start.26 = (f32[16,128]{1,0:T(8,128)S(1)}, f32[16,128]{1,0:T(8,128)S(1)}, u32[]{:S(2)}, u32[]{:S(2)}) collective-permute-start(f32[16,128]{1,0:T(8,128)S(1)} %get-tuple-element.32), channel_id=1, source_target_pairs={{0,192},{64,0},{128,64},{192,128},{1,193},{65,1},{129,65},{193,129... | collective-permute-start | bytes 24584 | tf_op jit(solution)/shard_map/ppermute | solution.py:26
  87.2 2.2 %collective-permute-start.24 = (f32[8,128]{1,0:T(8,128)S(1)}, f32[8,128]{1,0:T(8,128)S(1)}, u32[]{:S(2)}, u32[]{:S(2)}) collective-permute-start(f32[8,128]{1,0:T(8,128)S(1)} %pad_maximum_fusion.8), channel_id=1, source_target_pairs={{0,6},{2,4},{4,2},{6,0},{8,14},{10,12},{12,10},{14,8},{16,22},{18,... | collective-permute-start | bytes 12296 | tf_op jit(solution)/shard_map/ppermute | solution.py:319
  91.8 3.4 %collective-permute-done.28 = f32[16,128]{1,0:T(8,128)S(1)} collective-permute-done((f32[16,128]{1,0:T(8,128)S(1)}, f32[16,128]{1,0:T(8,128)S(1)}, u32[]{:S(2)}, u32[]{:S(2)}) %collective-permute-start.28) | collective-permute-done | bytes 8224 | tf_op jit(solution)/shard_map/ppermute | solution.py:26
  95.2 2.5 %shard_map.51 = f32[512,1024]{1,0:T(8,128)} custom-call(f32[512,512]{1,0:T(8,128)S(1)} %get-tuple-element.25.refs_12_.same_ref, f32[512,512]{1,0:T(8,128)S(1)} %get-tuple-element.29.other_ref, f32[512,128]{1,0:T(8,128)S(1)} %get-tuple-element.24.refs_4_.refs_10_.inv_ref, f32[8,128]{1,0:T(8,128)S(1)} %get-tuple-element.30.tinv_ref, ...), custom_call_target="tpu_custom_call" | custom-call | tf_op jit(solution)/shard_map/pallas_call | solution.py:265
  (72 shorter events, 18.6 us)
Async XLA Ops:
  7.8 11.6 %collective-permute-start.4 = (f32[2,144,128]{2,1,0:T(8,128)S(1)}, f32[2,144,128]{2,1,0:T(8,128)S(1)}, u32[]{:S(2)}, u32[]{:S(2)}) collective-permute-start(f32[2,144,128]{2,1,0:T(8,128)S(1)} %pad_maximum_fusion.4), channel_id=1, source_target_pairs={{0,8},{4,12},{8,16},{12,20},{16,24},{20,28},{24,0},{28,4},{1,9},{5... | collective-permute-start | bytes 442376 | tf_op jit(solution)/shard_map/ppermute | solution.py:26
  10.9 13.4 %collective-permute-start.5 = (f32[2,144,128]{2,1,0:T(8,128)S(1)}, f32[2,144,128]{2,1,0:T(8,128)S(1)}, u32[]{:S(2)}, u32[]{:S(2)}) collective-permute-start(f32[2,144,128]{2,1,0:T(8,128)S(1)} %pad_maximum_fusion.4), channel_id=1, source_target_pairs={{0,24},{4,28},{8,0},{12,4},{16,8},{20,12},{24,16},{28,20},{1,25},{... | collective-permute-start | bytes 442376 | tf_op jit(solution)/shard_map/ppermute | solution.py:26
  14.0 19.1 %collective-permute-start.12 = (f32[88,1024]{1,0:T(8,128)}, f32[88,1024]{1,0:T(8,128)S(1)}, u32[]{:S(2)}, u32[]{:S(2)}) collective-permute-start(f32[88,1024]{1,0:T(8,128)} %get-tuple-element.27), channel_id=1, source_target_pairs={{0,32},{32,0},{1,33},{33,1},{2,34},{34,2},{3,35},{35,3},{4,36},{36... | collective-permute-start | bytes 1081352 | tf_op jit(solution)/shard_map/ppermute | solution.py:26
  16.2 22.6 %collective-permute-start = (f32[128,1024]{1,0:T(8,128)}, f32[128,1024]{1,0:T(8,128)S(1)}, u32[]{:S(2)}, u32[]{:S(2)}) collective-permute-start(f32[128,1024]{1,0:T(8,128)} %tgt_ref.1), channel_id=1, source_target_pairs={{0,64},{64,128},{128,192},{192,0},{1,65},{65,129},{129,193},{193,1... | collective-permute-start | bytes 1572872 | tf_op jit(solution)/shard_map/ppermute | solution.py:26
  17.7 23.6 %collective-permute-start.1 = (f32[128,1024]{1,0:T(8,128)}, f32[128,1024]{1,0:T(8,128)S(1)}, u32[]{:S(2)}, u32[]{:S(2)}) collective-permute-start(f32[128,1024]{1,0:T(8,128)} %tgt_ref.1), channel_id=1, source_target_pairs={{0,192},{64,0},{128,64},{192,128},{1,193},{65,1},{129,65},{193,129... | collective-permute-start | bytes 1572872 | tf_op jit(solution)/shard_map/ppermute | solution.py:26
  19.4 10.9 %collective-permute-start.6 = (f32[2,144,128]{2,1,0:T(8,128)S(1)}, f32[2,144,128]{2,1,0:T(8,128)S(1)}, u32[]{:S(2)}, u32[]{:S(2)}) collective-permute-start(f32[2,144,128]{2,1,0:T(8,128)S(1)} %pad_maximum_fusion.4), channel_id=1, source_target_pairs={{0,16},{4,20},{8,24},{12,28},{16,0},{20,4},{24,8},{28,12},{1,17},{... | collective-permute-start | bytes 442376 | tf_op jit(solution)/shard_map/ppermute | solution.py:26
  24.4 13.5 %collective-permute-start.7 = (f32[4,144,128]{2,1,0:T(8,128)S(1)}, f32[4,144,128]{2,1,0:T(8,128)S(1)}, u32[]{:S(2)}, u32[]{:S(2)}) collective-permute-start(f32[4,144,128]{2,1,0:T(8,128)S(1)} %get-tuple-element.44), channel_id=1, source_target_pairs={{0,4},{4,8},{8,12},{12,16},{16,20},{20,24},{24,28},{28,0},{1,5},{5... | collective-permute-start | bytes 884744 | tf_op jit(solution)/shard_map/ppermute | solution.py:26
  30.3 15.4 %collective-permute-start.2 = (f32[128,1024]{1,0:T(8,128)}, f32[128,1024]{1,0:T(8,128)S(1)}, u32[]{:S(2)}, u32[]{:S(2)}) collective-permute-start(f32[128,1024]{1,0:T(8,128)} %tgt_ref.1), channel_id=1, source_target_pairs={{0,128},{64,192},{128,0},{192,64},{1,129},{65,193},{129,1},{193,65... | collective-permute-start | bytes 1572872 | tf_op jit(solution)/shard_map/ppermute | solution.py:26
  33.1 9.0 %collective-permute-start.8 = (f32[4,144,128]{2,1,0:T(8,128)S(1)}, f32[4,144,128]{2,1,0:T(8,128)S(1)}, u32[]{:S(2)}, u32[]{:S(2)}) collective-permute-start(f32[4,144,128]{2,1,0:T(8,128)S(1)} %get-tuple-element.43), channel_id=1, source_target_pairs={{0,28},{4,0},{8,4},{12,8},{16,12},{20,16},{24,20},{28,24},{1,29},{... | collective-permute-start | bytes 884744 | tf_op jit(solution)/shard_map/ppermute | solution.py:26
  37.9 15.4 %collective-permute-start.14 = (f32[88,1024]{1,0:T(8,128)S(1)}, f32[88,1024]{1,0:T(8,128)S(1)}, u32[]{:S(2)}, u32[]{:S(2)}) collective-permute-start(f32[88,1024]{1,0:T(8,128)S(1)} %select_maximum_fusion.refs_1_), channel_id=1, source_target_pairs={{0,64},{64,128},{128,192},{192,0},{1,65},{65,129},{129,193},{193,1... | collective-permute-start | bytes 1081352 | tf_op jit(solution)/shard_map/ppermute | solution.py:26
  38.8 15.6 %collective-permute-start.15 = (f32[88,1024]{1,0:T(8,128)S(1)}, f32[88,1024]{1,0:T(8,128)S(1)}, u32[]{:S(2)}, u32[]{:S(2)}) collective-permute-start(f32[88,1024]{1,0:T(8,128)S(1)} %select_maximum_fusion.refs_1_), channel_id=1, source_target_pairs={{0,192},{64,0},{128,64},{192,128},{1,193},{65,1},{129,65},{193,129... | collective-permute-start | bytes 1081352 | tf_op jit(solution)/shard_map/ppermute | solution.py:26
  41.3 17.1 %collective-permute-start.17 = (f32[88,1024]{1,0:T(8,128)S(1)}, f32[88,1024]{1,0:T(8,128)S(1)}, u32[]{:S(2)}, u32[]{:S(2)}) collective-permute-start(f32[88,1024]{1,0:T(8,128)S(1)} %select_maximum_fusion.refs_1_), channel_id=1, source_target_pairs={{0,128},{64,192},{128,0},{192,64},{1,129},{65,193},{129,1},{193,65... | collective-permute-start | bytes 1081352 | tf_op jit(solution)/shard_map/ppermute | solution.py:26
  42.1 19.9 %collective-permute-start.13 = (f32[96,1024]{1,0:T(8,128)S(1)}, f32[96,1024]{1,0:T(8,128)S(1)}, u32[]{:S(2)}, u32[]{:S(2)}) collective-permute-start(f32[96,1024]{1,0:T(8,128)S(1)} %pad_maximum_fusion.1), channel_id=1, source_target_pairs={{0,32},{32,0},{1,33},{33,1},{2,34},{34,2},{3,35},{35,3},{4,36},{36... | collective-permute-start | bytes 1179656 | tf_op jit(solution)/shard_map/ppermute | solution.py:26
  45.7 16.3 %collective-permute-start.9 = (f32[8,144,128]{2,1,0:T(8,128)S(1)}, f32[8,144,128]{2,1,0:T(8,128)S(1)}, u32[]{:S(2)}, u32[]{:S(2)}) collective-permute-start(f32[8,144,128]{2,1,0:T(8,128)S(1)} %pad_maximum_fusion.refs_0_), channel_id=1, source_target_pairs={{0,1},{1,0},{2,3},{3,2},{4,5},{5,4},{6,7},{7,6},{8,9},{9,8},{10,11... | collective-permute-start | bytes 1769480 | tf_op jit(solution)/shard_map/ppermute | solution.py:26
  53.3 8.7 %collective-permute-start.10 = (f32[8,144,128]{2,1,0:T(8,128)S(1)}, f32[8,144,128]{2,1,0:T(8,128)S(1)}, u32[]{:S(2)}, u32[]{:S(2)}) collective-permute-start(f32[8,144,128]{2,1,0:T(8,128)S(1)} %constant_dynamic-update-slice_fusion.refs_1_), channel_id=1, source_target_pairs={{0,1},{1,0},{2,3},{3,2},{4,5},{5,4},{6,7},{7,6},{8,9},{9,8},{10,11... | collective-permute-start | bytes 1769480 | tf_op jit(solution)/shard_map/ppermute | solution.py:26
  54.4 10.2 %collective-permute-start.11 = (f32[48,1024]{1,0:T(8,128)S(1)}, f32[48,1024]{1,0:T(8,128)S(1)}, u32[]{:S(2)}, u32[]{:S(2)}) collective-permute-start(f32[48,1024]{1,0:T(8,128)S(1)} %copy-done.2), channel_id=1, source_target_pairs={{0,32},{32,0},{1,33},{33,1},{2,34},{34,2},{3,35},{35,3},{4,36},{36... | collective-permute-start | bytes 589832 | tf_op jit(solution)/shard_map/ppermute | solution.py:26
  58.5 8.5 %collective-permute-start.16 = (f32[48,1024]{1,0:T(8,128)S(1)}, f32[48,1024]{1,0:T(8,128)S(1)}, u32[]{:S(2)}, u32[]{:S(2)}) collective-permute-start(f32[48,1024]{1,0:T(8,128)S(1)} %slice.174), channel_id=1, source_target_pairs={{0,32},{32,0},{1,33},{33,1},{2,34},{34,2},{3,35},{35,3},{4,36},{36... | collective-permute-start | bytes 589832 | tf_op jit(solution)/shard_map/ppermute | solution.py:26
  71.4 13.3 %collective-permute-start.19 = (f32[8,128]{1,0:T(8,128)S(1)}, f32[8,128]{1,0:T(8,128)S(1)}, u32[]{:S(2)}, u32[]{:S(2)}) collective-permute-start(f32[8,128]{1,0:T(8,128)S(1)} %pad_maximum_fusion.7), channel_id=1, source_target_pairs={{0,8},{4,12},{8,16},{12,20},{16,24},{20,28},{24,0},{28,4},{1,9},{5... | collective-permute-start | bytes 12296 | tf_op jit(solution)/shard_map/ppermute | solution.py:26
  77.8 8.0 %collective-permute-start.20 = (f32[8,128]{1,0:T(8,128)S(1)}, f32[8,128]{1,0:T(8,128)S(1)}, u32[]{:S(2)}, u32[]{:S(2)}) collective-permute-start(f32[8,128]{1,0:T(8,128)S(1)} %pad_maximum_fusion.7), channel_id=1, source_target_pairs={{0,24},{4,28},{8,0},{12,4},{16,8},{20,12},{24,16},{28,20},{1,25},{... | collective-permute-start | bytes 12296 | tf_op jit(solution)/shard_map/ppermute | solution.py:26
  77.8 8.0 %collective-permute-start.21 = (f32[8,128]{1,0:T(8,128)S(1)}, f32[8,128]{1,0:T(8,128)S(1)}, u32[]{:S(2)}, u32[]{:S(2)}) collective-permute-start(f32[8,128]{1,0:T(8,128)S(1)} %pad_maximum_fusion.7), channel_id=1, source_target_pairs={{0,16},{4,20},{8,24},{12,28},{16,0},{20,4},{24,8},{28,12},{1,17},{... | collective-permute-start | bytes 12296 | tf_op jit(solution)/shard_map/ppermute | solution.py:26
  81.5 5.8 %collective-permute-start.25 = (f32[16,128]{1,0:T(8,128)S(1)}, f32[16,128]{1,0:T(8,128)S(1)}, u32[]{:S(2)}, u32[]{:S(2)}) collective-permute-start(f32[16,128]{1,0:T(8,128)S(1)} %get-tuple-element.32), channel_id=1, source_target_pairs={{0,64},{64,128},{128,192},{192,0},{1,65},{65,129},{129,193},{193,1... | collective-permute-start | bytes 24584 | tf_op jit(solution)/shard_map/ppermute | solution.py:26
  82.2 7.2 %collective-permute-start.26 = (f32[16,128]{1,0:T(8,128)S(1)}, f32[16,128]{1,0:T(8,128)S(1)}, u32[]{:S(2)}, u32[]{:S(2)}) collective-permute-start(f32[16,128]{1,0:T(8,128)S(1)} %get-tuple-element.32), channel_id=1, source_target_pairs={{0,192},{64,0},{128,64},{192,128},{1,193},{65,1},{129,65},{193,129... | collective-permute-start | bytes 24584 | tf_op jit(solution)/shard_map/ppermute | solution.py:26
  85.8 5.9 %collective-permute-start.22 = (f32[8,128]{1,0:T(8,128)S(1)}, f32[8,128]{1,0:T(8,128)S(1)}, u32[]{:S(2)}, u32[]{:S(2)}) collective-permute-start(f32[8,128]{1,0:T(8,128)S(1)} %pad_maximum_fusion.8), channel_id=1, source_target_pairs={{0,4},{4,0},{8,12},{12,8},{16,20},{20,16},{24,28},{28,24},{1,5},{5... | collective-permute-start | bytes 12296 | tf_op jit(solution)/shard_map/ppermute | solution.py:318
  86.4 5.3 %collective-permute-start.23 = (f32[8,128]{1,0:T(8,128)S(1)}, f32[8,128]{1,0:T(8,128)S(1)}, u32[]{:S(2)}, u32[]{:S(2)}) collective-permute-start(f32[8,128]{1,0:T(8,128)S(1)} %pad_maximum_fusion.8), channel_id=1, source_target_pairs={{0,2},{2,0},{1,3},{3,1},{4,6},{6,4},{5,7},{7,5},{8,10},{10,8},{9,1... | collective-permute-start | bytes 12296 | tf_op jit(solution)/shard_map/ppermute | solution.py:26
  (8 other events, 92.2 us)
